TPU v7x, 32 devices: a whole 2x2x4 slice. The times are simulated.
32 devices in a mesh: band: 4 (over y, x), dx: 4 (over z), dy: 2 (over core).
Axes of the slice: x: 2, y: 2, z: 4, core: 2. Of those that a mesh axis runs over, the one named last changes fastest.
Arguments:
- wave_bands: float32 [4, 32, 32, 128], P('band', 'dx', 'dy'), may hold values from -6 to 6
- potential: float32 [32, 32, 128], P('dx', 'dy', 'band'), may hold values from -1.5 to 0.5
- atom_offsets: int32 [4, 2, 4, 3], P('dx', 'dy'), may hold values from 0 to 95, as said below
- proj_counts: int32 [4, 2, 4], P('dx', 'dy'), may hold values from 0 to 9, as said below
- dh_matrix: float32 [4, 2, 4, 9, 9], P('dx', 'dy'), as said below
- ds_matrix: float32 [4, 2, 4, 9, 9], P('dx', 'dy'), as said below
Outputs:
- new_bands: float32 [4, 32, 32, 128], P('band', 'dx', 'dy')
- new_residual: float32 [4, 32, 32, 128], P('band', 'dx', 'dy')
- band_energy: float32 [4], P('band')
Inputs may be any that keep to these rules, and one draw needn't show every extreme that they name: `atom_offsets`: columns are x in 0..7, y in 0..15, z in 32..3*128/4-1. `proj_counts`: each count is 0 (empty slot), 1, 4 or 9. `dh_matrix`: each matrix is symmetric. `ds_matrix`: each matrix is symmetric, and each diagonal entry exceeds the sum of the magnitudes of the other entries in its row.
All inputs are finite; a program needn't handle non-finite values.
Results may differ from a plain program's by a relative error of at most 0.00017.
Values sent between devices are 32-bit elements; how exact they have to be, the bound alone decides.
No kernel may reach another device: no remote copies, remote signals or barrier semaphores. Data moves between devices by JAX's collectives and lax.ppermute only.
A program may use at most 64 MiB of HBM per device.

v0:
```python
import functools

import jax
import jax.numpy as jnp
from jax import lax
from jax.experimental import pallas as pl
from jax.experimental.pallas import tpu as pltpu
from jax.sharding import PartitionSpec as P

NPROJ = 9
COARSE_SWEEPS = 2


STENCIL = (-49.0 / 18.0, 1.5, -0.15, 1.0 / 90.0)
RELAXATION = 2.0 / 3.0
MASS_SHIFT = 0.25
AMPLITUDE = 0.15
PRECISE = lax.Precision.HIGHEST


def extended(cells, sides, width):
    for axis, dim in sides:
        count = lax.axis_size(axis)
        head = lax.slice_in_dim(cells, 0, width, axis=dim)
        tail = lax.slice_in_dim(cells, cells.shape[dim] - width, cells.shape[dim], axis=dim)
        cells = jnp.concatenate(
            [
                lax.ppermute(tail, axis, [(i, (i + 1) % count) for i in range(count)]),
                cells,
                lax.ppermute(head, axis, [((i + 1) % count, i) for i in range(count)]),
            ],
            axis=dim,
        )
    return cells


def projector_table():
    box_steps = jnp.arange(12, dtype=jnp.float32) - 6.0
    filler = jnp.ones((12, 12, 12), jnp.float32)
    along_x = box_steps[:, None, None] * filler
    along_y = box_steps[None, :, None] * filler
    along_z = box_steps[None, None, :] * filler
    radius_sq = along_x * along_x + along_y * along_y + along_z * along_z
    radial_s = jnp.exp(-radius_sq / 8.0)
    radial_p = jnp.exp(-radius_sq / 9.68) / 2.2
    radial_d = jnp.exp(-radius_sq / 11.52) / 5.76
    angular = [
        radial_s,
        radial_p * along_x,
        radial_p * along_y,
        radial_p * along_z,
        radial_d * along_x * along_y,
        radial_d * along_y * along_z,
        radial_d * along_z * along_x,
        0.5 * radial_d * (along_x * along_x - along_y * along_y),
        radial_d * (3.0 * along_z * along_z - radius_sq) * 0.28867513,
    ]
    return AMPLITUDE * jnp.stack(angular).reshape(9, 1728)


def shift_z(field, reach):
    depth = field.shape[-1]
    zeros_rim = jnp.zeros(field.shape[:-1] + (abs(reach),), field.dtype)
    if reach > 0:
        return jnp.concatenate([zeros_rim, field[..., : depth - reach]], axis=-1)
    return jnp.concatenate([field[..., -reach:], zeros_rim], axis=-1)


def kinetic_padded(padded, width, tile_x, tile_y):
    center = padded[:, width : width + tile_x, width : width + tile_y]
    laplacian = 3.0 * STENCIL[0] * center
    for reach in (1, 2, 3):
        weight = STENCIL[reach]
        laplacian = laplacian + weight * (
            padded[:, width - reach : width - reach + tile_x, width : width + tile_y]
            + padded[:, width + reach : width + reach + tile_x, width : width + tile_y]
            + padded[:, width : width + tile_x, width - reach : width - reach + tile_y]
            + padded[:, width : width + tile_x, width + reach : width + reach + tile_y]
            + shift_z(center, reach)
            + shift_z(center, -reach)
        )
    return -0.5 * laplacian


def box_targets(places, tile_x, tile_y, depth):
    box_steps = jnp.arange(12, dtype=jnp.int32)
    tile_shift = jnp.arange(3, dtype=jnp.int32) - 1
    target_x = (
        tile_shift[:, None, None, None] * tile_x + places[:, :, :, 0][..., None] - 6 + box_steps
    )
    target_y = (
        tile_shift[None, :, None, None] * tile_y + places[:, :, :, 1][..., None] - 6 + box_steps
    )
    target_z = places[:, :, :, 2][..., None] - 6 + box_steps
    target_x = jnp.where((target_x >= 0) & (target_x < tile_x), target_x, tile_x + 12)
    target_y = jnp.where((target_y >= 0) & (target_y < tile_y), target_y, tile_y + 12)
    depth_cells = jnp.arange(depth, dtype=jnp.int32)
    window = (target_z[..., None] == depth_cells).astype(jnp.float32)
    return (target_x, target_y, window)


def own_intersection(widened, atom_offsets, window, projector_rows):
    nbands = widened.shape[0]
    box_steps = jnp.arange(12, dtype=jnp.int32)
    owned = atom_offsets[0, 0]
    index_x = (owned[:, 0:1] + box_steps[None, :])[:, :, None]
    index_y = (owned[:, 1:2] + box_steps[None, :])[:, None, :]
    columns = widened[:, index_x, index_y]
    box_values = jnp.einsum("bauvz,akz->bauvk", columns, window[1, 1], precision=PRECISE)
    box_values = box_values.reshape(nbands, -1, 1728)
    return jnp.einsum("ik,bak->aib", projector_rows, box_values, precision=PRECISE)


def projector_terms(
    intersection, proj_counts, targets, dh_matrix, ds_matrix, projector_rows, field_shape
):
    nbands, tile_x, tile_y, depth = field_shape
    active = (jnp.arange(NPROJ, dtype=jnp.int32)[None, :] < proj_counts[0, 0][:, None]).astype(
        jnp.float32
    )
    intersection = intersection * active[:, :, None]
    coefficients = jnp.stack(
        [
            jnp.einsum("aij,ajb->aib", dh_matrix[0, 0], intersection, precision=PRECISE),
            jnp.einsum("aij,ajb->aib", ds_matrix[0, 0], intersection, precision=PRECISE),
        ]
    )
    coefficients = coefficients * active[None, :, :, None]
    nearby = extended(coefficients[None, None], (("dx", 0), ("dy", 1)), 1)
    spread = jnp.einsum("ik,uvhaib->hbuvak", projector_rows, nearby, precision=PRECISE)
    spread = spread.reshape(2, nbands, 3, 3, -1, 144, 12)
    target_x, target_y, window = targets
    placed = jnp.einsum("hbuvaxk,uvakz->hbuvaxz", spread, window, precision=PRECISE)
    placed = placed.reshape(2, nbands, 3, 3, -1, 12, 12, depth)
    correction = jnp.zeros((2, nbands, tile_x, tile_y, depth), jnp.float32)
    correction = correction.at[:, :, target_x[..., :, None], target_y[..., None, :]].add(
        placed, mode="drop"
    )
    return (correction[0], correction[1])


def hamiltonian(
    field, full_potential, atom_offsets, proj_counts, targets, dh_matrix, ds_matrix, projector_rows
):
    tile_x, tile_y = (field.shape[1], field.shape[2])
    widened = extended(field, (("dx", 1), ("dy", 2)), 6)
    kinetic_part = kinetic_padded(widened, 6, tile_x, tile_y)
    intersection = own_intersection(widened, atom_offsets, targets[2], projector_rows)
    corr_h, corr_s = projector_terms(
        intersection, proj_counts, targets, dh_matrix, ds_matrix, projector_rows, field.shape
    )
    return (kinetic_part + full_potential[None] * field + corr_h, field + corr_s)


def domain_sums(values):
    return lax.psum(values, ("dx", "dy"))


def diagonal_of(level):
    return 3.0 / 4.0**level + MASS_SHIFT


def tile_apply(field, level):
    padded = extended(field, (("dx", 1), ("dy", 2)), 1)
    neighbours = (
        padded[:, :-2, 1:-1]
        + padded[:, 2:, 1:-1]
        + padded[:, 1:-1, :-2]
        + padded[:, 1:-1, 2:]
        + shift_z(field, 1)
        + shift_z(field, -1)
    )
    return -0.5 * (neighbours - 6.0 * field) / 4.0**level + MASS_SHIFT * field


def pair_table(depth):
    fine_cells = jnp.arange(depth, dtype=jnp.int32)[:, None] // 2
    coarse_cells = jnp.arange(depth // 2, dtype=jnp.int32)[None, :]
    return (fine_cells == coarse_cells).astype(jnp.float32)


def restrict(field):
    nbands, size_x, size_y, size_z = field.shape
    planar = field.reshape(nbands, size_x // 2, 2, size_y // 2, 2, size_z).mean(axis=(2, 4))
    return jnp.einsum("bxyz,zw->bxyw", planar, 0.5 * pair_table(size_z), precision=PRECISE)


def prolong(field):
    size_z = field.shape[3]
    widened = jnp.repeat(jnp.repeat(field, 2, axis=1), 2, axis=2)
    return jnp.einsum("bxyw,zw->bxyz", widened, pair_table(2 * size_z), precision=PRECISE)


def precondition(source_zero):
    guess_zero = RELAXATION * source_zero / diagonal_of(0)
    source_one = restrict(source_zero - tile_apply(guess_zero, 0))
    guess_one = RELAXATION * source_one / diagonal_of(1)
    source_two = restrict(source_one - tile_apply(guess_one, 1))
    guess_two = RELAXATION * source_two / diagonal_of(2)
    for _ in range(COARSE_SWEEPS):
        guess_two = guess_two + RELAXATION * (source_two - tile_apply(guess_two, 2)) / diagonal_of(
            2
        )
    guess_one = guess_one + prolong(guess_two)
    guess_one = guess_one + RELAXATION * (source_one - tile_apply(guess_one, 1)) / diagonal_of(1)
    guess_zero = guess_zero + prolong(guess_one)
    return guess_zero + RELAXATION * (source_zero - tile_apply(guess_zero, 0)) / diagonal_of(0)


def distributed(wave_bands, potential, atom_offsets, proj_counts, dh_matrix, ds_matrix):
    projector_rows = projector_table()
    full_potential = lax.all_gather(potential, "band", axis=2, tiled=True)
    places = extended(atom_offsets, (("dx", 0), ("dy", 1)), 1)
    targets = box_targets(places, wave_bands.shape[1], wave_bands.shape[2], wave_bands.shape[3])
    h_band, s_band = hamiltonian(
        wave_bands,
        full_potential,
        atom_offsets,
        proj_counts,
        targets,
        dh_matrix,
        ds_matrix,
        projector_rows,
    )
    energy_sums = domain_sums(
        jnp.stack(
            [
                jnp.sum(wave_bands * h_band, axis=(1, 2, 3)),
                jnp.sum(wave_bands * s_band, axis=(1, 2, 3)),
            ]
        )
    )
    band_energy = energy_sums[0] / energy_sums[1]
    energy_grid = band_energy[:, None, None, None]
    residual = h_band - energy_grid * s_band
    direction = precondition(residual)
    h_dir, s_dir = hamiltonian(
        direction,
        full_potential,
        atom_offsets,
        proj_counts,
        targets,
        dh_matrix,
        ds_matrix,
        projector_rows,
    )
    change = h_dir - energy_grid * s_dir
    line_sums = domain_sums(
        jnp.stack(
            [jnp.sum(residual * change, axis=(1, 2, 3)), jnp.sum(change * change, axis=(1, 2, 3))]
        )
    )
    step_grid = (-line_sums[0] / line_sums[1])[:, None, None, None]
    return (wave_bands + step_grid * direction, residual + step_grid * change, band_energy)


BOX_LOW = 6
BOX_CELLS = 12
LANES = 128
SUBLANES = 8
RADIAL_WIDTHS = (8.0, 9.68, 11.52)
PLANE_FACTORS = (
    (0, 0, 0),
    (1, 1, 0),
    (1, 0, 1),
    (1, 0, 0),
    (2, 1, 1),
    (2, 0, 1),
    (2, 1, 0),
    (2, 2, 0),
    (2, 0, 0),
    (2, 0, 2),
)
D_SCALE = 0.28867513
DEPTH_SCALE = 180.0
BLOCK = 8
VMEM_BUDGET = 40 * 1024 * 1024
VMEM_GRANT = 24 * 1024 * 1024


class Sizes:
    def __init__(self, wave, potential, atoms, tiles_x, tiles_y, groups):
        self.tile_x, self.tile_y, self.depth = wave.shape[1:]
        self.atoms = atoms
        self.tiles_x, self.tiles_y, self.groups = tiles_x, tiles_y, groups
        self.grid_x, self.grid_y = tiles_x * self.tile_x, tiles_y * self.tile_y
        self.cells = self.grid_x * self.grid_y
        self.chunk = potential.shape[2]
        self.all_atoms = tiles_x * tiles_y * atoms
        self.wave_rows = self.tile_x * self.tile_y
        self.pot_rows = self.wave_rows // groups
        self.param_rows = -(-2 * atoms // SUBLANES) * SUBLANES
        self.rows = self.wave_rows + self.pot_rows + self.param_rows
        self.factors = len(PLANE_FACTORS) * self.all_atoms

    def fits(self, vmem_bytes):
        return (
            self.depth == LANES
            and self.chunk * self.groups == LANES
            and self.tile_x % max(self.groups, BLOCK) == 0
            and self.tile_y % 16 == 0
            and self.grid_x >= 2 * BLOCK
            and self.grid_y >= 32
            and self.all_atoms % 16 == 0
            and LANES % self.all_atoms == 0
            and self.cells * (60 * LANES + 8 * self.factors) <= vmem_bytes
        )


def lanes_of(rows=1):
    return lax.broadcasted_iota(jnp.int32, (rows, LANES), 1)


def split(value):
    high = value.astype(jnp.bfloat16)
    return high, (value - high.astype(jnp.float32)).astype(jnp.bfloat16)


def halves(value):
    return value[:, :LANES] + value[:, LANES:]


def dot(left, right):
    return jnp.dot(left, right, preferred_element_type=jnp.float32)


META_LANE = 96


def pack_kernel(sz, wave_ref, pot_ref, offs_ref, counts_ref, dh_ref, ds_ref, out_ref, *scratch):
    *places, sems = scratch
    pot, offs, counts, dh, ds = places
    start, base = sz.wave_rows, sz.wave_rows + sz.pot_rows
    sources = (pot_ref, offs_ref, counts_ref, dh_ref, ds_ref, wave_ref)
    places = places + [out_ref.at[pl.ds(0, start)]]
    copies = [
        pltpu.make_async_copy(a, b, sems.at[i])
        for i, (a, b) in enumerate(zip(sources, places))
    ]
    for copy in copies:
        copy.start()
    out_ref[base:, :] = jnp.zeros((sz.param_rows, LANES), jnp.float32)
    for copy in copies:
        copy.wait()
    per = sz.tile_x // sz.groups
    pieces = [
        pot[g * per : (g + 1) * per].reshape(sz.pot_rows, sz.chunk) for g in range(sz.groups)
    ]
    out_ref[start:base, :] = pltpu.roll(
        jnp.concatenate(pieces, axis=1), lax.axis_index("band") * sz.chunk, 1
    )
    for j in range(NPROJ):
        lanes = slice(j * NPROJ, (j + 1) * NPROJ)
        out_ref[base : base + sz.atoms, lanes] = dh[0, 0, j]
        out_ref[base + sz.atoms : base + 2 * sz.atoms, lanes] = ds[0, 0, j]
    lane = lanes_of(1)
    for a in range(sz.atoms):
        row = jnp.where(lane == META_LANE + 3, counts[0, 0, a].astype(jnp.float32), 0.0)
        for k in range(3):
            row = jnp.where(lane == META_LANE + k, offs[0, k, 0, a].astype(jnp.float32), row)
        out_ref[base + a : base + a + 1, META_LANE : META_LANE + 4] = row[:, META_LANE : META_LANE + 4]


def wrapped(cell, centre, count):
    offset = cell - centre + float(BOX_LOW)
    offset = jnp.where(offset < 0.0, offset + float(count), offset)
    offset = jnp.where(offset >= float(count), offset - float(count), offset)
    inside = offset < float(BOX_CELLS)
    return offset - float(BOX_LOW), inside


def fill_rims(ref, width, count_x, count_y):
    ref[:, 0:SUBLANES, :] = ref[:, count_y : count_y + SUBLANES, :]
    ref[:, count_y + SUBLANES : count_y + 2 * SUBLANES, :] = ref[:, SUBLANES : 2 * SUBLANES, :]
    ref[0:width] = ref[count_x : count_x + width]
    ref[count_x + width : count_x + 2 * width] = ref[width : 2 * width]


def shifted_pair(value, reach):
    lane = lanes_of(1)
    below = jnp.where(lane >= reach, pltpu.roll(value, reach, 1), 0.0)
    above = jnp.where(lane < LANES - reach, pltpu.roll(value, LANES - reach, 1), 0.0)
    return below + above


def planar_kinetic(ref, x0, y0, rows, count):
    at = lambda x, y: ref[x0 + x + 3, pl.ds(SUBLANES + y0 + y, rows), :]
    planes = [at(x, 0) for x in range(-3, count + 3)]
    found = []
    for x in range(count):
        total = (-1.5 * STENCIL[0]) * planes[x + 3]
        for reach in (1, 2, 3):
            around = (planes[x + 3 - reach] + planes[x + 3 + reach]) + (at(x, -reach) + at(x, reach))
            total = total + (-0.5 * STENCIL[reach]) * around
        found.append((planes[x + 3], total))
    return found


def depth_matrix():
    row = lax.broadcasted_iota(jnp.int32, (2 * LANES, LANES), 0) % LANES
    reach = jnp.abs(row - lax.broadcasted_iota(jnp.int32, (2 * LANES, LANES), 1))
    value = jnp.zeros((2 * LANES, LANES), jnp.float32)
    for k in (1, 2, 3):
        value = jnp.where(reach == k, -0.5 * STENCIL[k] * DEPTH_SCALE, value)
    return value.astype(jnp.bfloat16)


def neighbour_block(ref, x0, y0, rows, count, step):
    at = lambda x, y: ref[x0 + x + 1, pl.ds(SUBLANES + y0 + y, rows), :]
    planes = [at(x, 0) for x in range(-1, count + 1)]
    found = []
    for x in range(count):
        center = planes[x + 1]
        around = (planes[x] + planes[x + 2]) + (at(x, -1) + at(x, 1)) + shifted_pair(center, step)
        found.append((center, around))
    return found


def over_blocks(count, body):
    if count <= 2 * BLOCK:
        for x0 in range(0, count, BLOCK):
            body(x0)
        return

    def step(index, carry):
        body(index * BLOCK)
        return carry

    lax.fori_loop(0, count // BLOCK, step, 0)


def plane_weights(sz, meta, w_ref, a_ref, wx_ref, wy_ref):
    atoms = sz.all_atoms
    widths = [-1.0 / w for w in RADIAL_WIDTHS]
    for tile in range(sz.cells // LANES):
        cell = lanes_of(1) + tile * LANES
        cell_x = (cell // sz.grid_y).astype(jnp.float32)
        cell_y = (cell % sz.grid_y).astype(jnp.float32)
        for start in range(0, atoms, 16):
            rx, inside_x = wrapped(cell_x, meta[start : start + 16, 0:1], sz.grid_x)
            ry, inside_y = wrapped(cell_y, meta[start : start + 16, 1:2], sz.grid_y)
            square = rx * rx + ry * ry
            inside = jnp.logical_and(inside_x, inside_y)
            radial = [jnp.where(inside, jnp.exp(square * w), 0.0) for w in widths]
            powers_x, powers_y = [None, rx, rx * rx], [None, ry, ry * ry]
            for index, (kind, px, py) in enumerate(PLANE_FACTORS):
                value = radial[kind]
                value = value if px == 0 else value * powers_x[px]
                value = value if py == 0 else value * powers_y[py]
                high, low = split(value)
                at = index * atoms + start
                lanes = slice(tile * LANES, (tile + 1) * LANES)
                w_ref[at : at + 16, lanes] = high
                w_ref[sz.factors + at : sz.factors + at + 16, lanes] = low
    turned = jnp.concatenate([meta] * (LANES // atoms), axis=0).T
    tiles = 2 * sz.factors // LANES
    for axis, count, ref in ((0, sz.grid_x, wx_ref), (1, sz.grid_y, wy_ref)):
        centre = turned[axis : axis + 1, :]
        cell = lax.broadcasted_iota(jnp.int32, (count, LANES), 0).astype(jnp.float32)
        offset, inside = wrapped(cell, centre, count)
        radial = [jnp.where(inside, jnp.exp(offset * offset * w), 0.0) for w in widths]
        powers = [1.0, offset, offset * offset]
        for tile in range(tiles):
            place = lanes_of(1) // atoms + tile * (LANES // atoms)
            value = None
            for slot in range(LANES // atoms):
                index = tile * (LANES // atoms) + slot
                kind, *power = PLANE_FACTORS[index % len(PLANE_FACTORS)]
                term = radial[kind] if power[axis] == 0 else radial[kind] * powers[power[axis]]
                value = term if value is None else jnp.where(place == index, term, value)
            ref[tile] = value

    def planes(x):
        rows = pl.ds(pl.multiple_of(x * sz.grid_y, 16), sz.grid_y)
        for tile in range(tiles):
            lanes = slice(tile * LANES, (tile + 1) * LANES)
            value = wx_ref[tile, pl.ds(x, 1), :] * wy_ref[tile]
            high = value.astype(jnp.bfloat16)
            if (tile + 1) * LANES > sz.factors:
                low = value - high.astype(jnp.float32)
                if tile * LANES < sz.factors:
                    low = jnp.where(lanes_of(1) + tile * LANES < sz.factors, value, low)
                high = low.astype(jnp.bfloat16)
            a_ref[rows, lanes] = high

    lax.fori_loop(0, sz.grid_x, lambda x, c: (planes(x), c)[1], 0, unroll=4)


def depth_weights(meta, wz_ref):
    offset = lanes_of(1).astype(jnp.float32) - meta[:, 2:3]
    inside = jnp.logical_and(offset >= -float(BOX_LOW), offset < float(BOX_CELLS - BOX_LOW))
    radial = [
        jnp.where(inside, (AMPLITUDE * scale) * jnp.exp(offset * offset * (-1.0 / w)), 0.0)
        for scale, w in zip((1.0, 1.0 / 2.2, 1.0 / 5.76), RADIAL_WIDTHS)
    ]
    wz_ref[0] = radial[0]
    wz_ref[1] = radial[1]
    wz_ref[2] = radial[1] * offset
    wz_ref[3] = radial[2]
    wz_ref[4] = radial[2] * offset
    wz_ref[5] = radial[2] * (offset * offset)


def intersections(sz, w_ref, parts, wz_ref, active):
    high, low = parts[:, :LANES], parts[:, LANES:]
    sums = dot(w_ref[: sz.factors], high)
    sums = sums + (dot(w_ref[: sz.factors], low) + dot(w_ref[sz.factors :], high))
    u = [sums[c * sz.all_atoms : (c + 1) * sz.all_atoms] for c in range(len(PLANE_FACTORS))]
    products = [
        u[0] * wz_ref[0],
        u[1] * wz_ref[1],
        u[2] * wz_ref[1],
        u[3] * wz_ref[2],
        u[4] * wz_ref[3],
        u[5] * wz_ref[4],
        u[6] * wz_ref[4],
        (0.5 * (u[7] - u[9])) * wz_ref[3],
        D_SCALE * (2.0 * u[8] * wz_ref[5] - (u[7] + u[9]) * wz_ref[3]),
    ]
    return [jnp.sum(p, axis=1, keepdims=True) * active[i] for i, p in enumerate(products)]


def active_columns(meta):
    return [(meta[:, 3:4] > float(i)).astype(jnp.float32) for i in range(NPROJ)]


def inner_lanes(columns):
    lane = lanes_of(1)
    inner = jnp.zeros((columns[0].shape[0], LANES), jnp.float32)
    for k in range(NPROJ):
        inner = jnp.where(jnp.logical_and(lane % NPROJ == k, lane < NPROJ * NPROJ), columns[k], inner)
    return inner


def projector_sources(sz, matrix, inner, active, wz_ref, q_ref):
    lane = lanes_of(1)
    terms = DEPTH_SCALE * (matrix * inner)
    coef = [
        jnp.sum(jnp.where(lane // NPROJ == i, terms, 0.0), axis=1, keepdims=True) * active[i]
        for i in range(NPROJ)
    ]
    tilt = (0.5 * coef[7]) * wz_ref[3]
    ring = (D_SCALE * coef[8]) * wz_ref[3]
    blocks = [
        coef[0] * wz_ref[0],
        coef[1] * wz_ref[1],
        coef[2] * wz_ref[1],
        coef[3] * wz_ref[2],
        coef[4] * wz_ref[3],
        coef[5] * wz_ref[4],
        coef[6] * wz_ref[4],
        tilt - ring,
        (2.0 * D_SCALE * coef[8]) * wz_ref[5],
        -(tilt + ring),
    ]
    for index, block in enumerate(blocks):
        at = index * sz.all_atoms
        high, low = split(block)
        q_ref[at : at + sz.all_atoms, :LANES] = high
        q_ref[at : at + sz.all_atoms, LANES:] = low
        q_ref[sz.factors + at : sz.factors + at + sz.all_atoms, :LANES] = high


def tile_at(sz, index):
    turn_y, turn_x = divmod(index, sz.tiles_x)
    tile_x = partner(lax.axis_index("dx"), turn_x, sz.tiles_x)
    tile_y = partner(lax.axis_index("dy"), turn_y, sz.tiles_y)
    return tile_x, tile_y


def add_projectors(sz, a_ref, q_ref, emit):
    part = sz.cells // 2
    for at in range(0, sz.cells, part):
        emit(at, part, halves(dot(a_ref[at : at + part, :], q_ref[...])))


def first_kernel(sz, *refs):
    blocks, refs = refs[: sz.tiles_x * sz.tiles_y], refs[sz.tiles_x * sz.tiles_y :]
    (psi, spsi, zkin, inner_ref, w_ref, a_ref, wz_ref, par_ref), refs = refs[:8], refs[8:]
    (parts, q_ref, wx_ref, wy_ref) = refs
    nx, ny = sz.grid_x, sz.grid_y
    for index, block in enumerate(blocks):
        tile_x, tile_y = tile_at(sz, index)
        at_y = pl.multiple_of(tile_y * sz.tile_y, 16)
        for x in range(sz.tile_x):
            value = block[x * sz.tile_y : (x + 1) * sz.tile_y, :]
            cell_x = tile_x * sz.tile_x + x
            psi[cell_x + 3, pl.ds(at_y + SUBLANES, sz.tile_y), :] = value
            rows = pl.ds(pl.multiple_of(cell_x * ny + at_y, 16), sz.tile_y)
            high, low = split(value)
            parts[rows, :LANES] = high
            parts[rows, LANES:] = low
        tile = tile_x * sz.tiles_y + tile_y
        for k in range(2):
            at = sz.wave_rows + sz.pot_rows + k * sz.atoms
            par_ref[k, pl.ds(tile * sz.atoms, sz.atoms), :] = block[at : at + sz.atoms, :]
    fill_rims(psi, 3, nx, ny)
    owners = lax.broadcasted_iota(jnp.int32, (sz.all_atoms, LANES), 0) // sz.atoms
    lane = lanes_of(sz.all_atoms)
    meta = pltpu.roll(par_ref[0], LANES - META_LANE, 1)
    meta = meta + jnp.where(lane == 0, (owners // sz.tiles_y * sz.tile_x).astype(jnp.float32), 0.0)
    meta = meta + jnp.where(lane == 1, (owners % sz.tiles_y * sz.tile_y).astype(jnp.float32), 0.0)
    par_ref[2] = meta
    depth_weights(meta, wz_ref)
    plane_weights(sz, meta, w_ref, a_ref, wx_ref, wy_ref)
    active = active_columns(meta)
    columns = intersections(sz, w_ref, parts[...], wz_ref, active)
    zkin[...] = dot(parts[...], depth_matrix())
    inner = inner_lanes(columns)
    inner_ref[...] = inner
    q_ref[sz.factors :, LANES:] = jnp.zeros((sz.factors, LANES), jnp.bfloat16)
    projector_sources(sz, par_ref[1], inner, active, wz_ref, q_ref)

    def emit_s(at, rows, value):
        x0, count = at // ny, rows // ny
        center = psi[x0 + 3 : x0 + 3 + count, SUBLANES : SUBLANES + ny, :]
        spsi[x0 : x0 + count] = center + (1.0 / DEPTH_SCALE) * value.reshape(count, ny, LANES)

    add_projectors(sz, a_ref, q_ref, emit_s)


def second_kernel(sz, *refs):
    (psi, spsi, zkin, inner_ref, a_ref, wz_ref, par_ref, hpsi, sums_ref, q_ref) = refs
    nx, ny = sz.grid_x, sz.grid_y
    q_ref[sz.factors :, LANES:] = jnp.zeros((sz.factors, LANES), jnp.bfloat16)
    active = active_columns(par_ref[2])
    projector_sources(sz, par_ref[0], inner_ref[...], active, wz_ref, q_ref)

    def emit_h(at, rows, value):
        x0, count = at // ny, rows // ny
        total = value + zkin[at : at + rows, :]
        hpsi[x0 : x0 + count] = (1.0 / DEPTH_SCALE) * total.reshape(count, ny, LANES)

    add_projectors(sz, a_ref, q_ref, emit_h)

    def block(index, carry):
        x0, (energy, norm) = index * BLOCK, carry
        for y0 in range(0, ny, SUBLANES):
            rows = pl.ds(y0, SUBLANES)
            for x, (center, value) in enumerate(planar_kinetic(psi, x0, y0, SUBLANES, BLOCK)):
                value = value + hpsi[x0 + x, rows, :]
                hpsi[x0 + x, rows, :] = value
                energy = energy + value * center
                norm = norm + spsi[x0 + x, rows, :] * center
        return energy, norm

    zero = jnp.zeros((SUBLANES, LANES), jnp.float32)
    energy, norm = lax.fori_loop(0, nx // BLOCK, block, (zero, zero))
    sums_ref[0:1, :] = jnp.sum(energy, axis=0, keepdims=True)
    sums_ref[1:2, :] = jnp.sum(norm, axis=0, keepdims=True)


def pair_lanes(value, step):
    lane = lanes_of(1)
    other = jnp.where(
        (lane // step) % 2 == 1, pltpu.roll(value, step, 1), pltpu.roll(value, LANES - step, 1)
    )
    return value + other


def level_numbers(level):
    return 0.5 / 4.0**level, RELAXATION / diagonal_of(level)


def restrict_into(count_x, count_y, level, source, target, rows_ref):
    spread, guess = level_numbers(level)
    rows = 2 * SUBLANES

    def body(x0):
        for y0 in range(0, count_y, rows):
            found = neighbour_block(source, x0, y0, rows, BLOCK, 2**level)
            values = [(1.0 - RELAXATION) * c + (spread * guess) * n for c, n in found]
            for x in range(BLOCK // 2):
                slot = y0 // rows * (BLOCK // 2) + x
                rows_ref[slot] = values[2 * x] + values[2 * x + 1]
                total = (
                    rows_ref[slot, pl.ds(0, SUBLANES, stride=2), :]
                    + rows_ref[slot, pl.ds(1, SUBLANES, stride=2), :]
                )
                target[x0 // 2 + x + 1, pl.ds(SUBLANES + y0 // 2, SUBLANES), :] = 0.125 * pair_lanes(
                    total, 2**level
                )

    over_blocks(count_x, body)
    fill_rims(target, 1, count_x // 2, count_y // 2)


def relax_rows(count_x, count_y, level, guess_ref, source, emit):
    spread, guess = level_numbers(level)
    rows = min(2 * SUBLANES, count_y)

    def body(x0):
        for y0 in range(0, count_y, rows):
            found = neighbour_block(guess_ref, x0, y0, rows, BLOCK, 2**level)
            for x, (center, around) in enumerate(found):
                right = source[x0 + x + 1, pl.ds(SUBLANES + y0, rows), :]
                value = (1.0 - RELAXATION) * center + guess * right + (guess * spread) * around
                emit(x0 + x, y0, rows, value)

    over_blocks(count_x, body)


def prolong_into(count_x, count_y, level, coarse, source, target):
    guess = level_numbers(level)[1]

    def body(x0):
        for y0 in range(0, count_y, 2 * SUBLANES):
            for half in range(BLOCK // 2):
                value = coarse(x0 // 2 + half, y0 // 2)
                for part in range(2):
                    at = x0 + 2 * half + part + 1
                    for row in range(2):
                        rows = pl.ds(SUBLANES + y0 + row, SUBLANES, stride=2)
                        target[at, rows, :] = value + guess * source[at, rows, :]

    over_blocks(count_x, body)
    fill_rims(target, 1, count_x, count_y)


def place_potential(sz, pots, psi, pot, sums):
    per = sz.tile_x // sz.groups
    slot = lanes_of(1) // sz.chunk
    here_group = lax.axis_index("band")
    for index in range(sz.tiles_x * sz.tiles_y):
        shift_y, shift_x = divmod(index, sz.tiles_x)
        tile_x, tile_y = tile_at(sz, index)
        at_y = pl.multiple_of(tile_y * sz.tile_y, 16)
        total = jnp.zeros((sz.tile_y, LANES), jnp.float32)
        for g in range(sz.groups):
            value = None
            for shift_b in range(sz.groups):
                source = partner(here_group, shift_b, sz.groups)
                at = (shift_b * sz.tiles_x + shift_x) * sz.pot_rows
                piece = pots[shift_y][at : at + sz.pot_rows, :]
                chosen = slot == lax.rem(source + g, sz.groups)
                value = piece if value is None else jnp.where(chosen, piece, value)
            if g:
                value = pltpu.roll(value, LANES - g * sz.chunk, 1)
            for k in range(per):
                cell_x = tile_x * sz.tile_x + g * per + k
                plane = value[k * sz.tile_y : (k + 1) * sz.tile_y]
                pot[cell_x, pl.ds(at_y, sz.tile_y), :] = plane
                center = psi[cell_x + 3, pl.ds(at_y + SUBLANES, sz.tile_y), :]
                total = total + plane * (center * center)
        sums[tile_x * sz.tiles_y + tile_y] = total
    total = sums[0]
    for tile in range(1, sz.tiles_x * sz.tiles_y):
        total = total + sums[tile]
    return total


def step_kernel(sz, *refs):
    pots, refs = refs[: sz.tiles_y], refs[sz.tiles_y :]
    (psi, hpsi, spsi, w_ref, a_ref, wz_ref, par_ref, sums_ref), refs = refs[:8], refs[8:]
    (bands_ref, resid_ref, energy_ref), refs = refs[:3], refs[3:]
    (pot, corr, res, zfield, direct, change, b1, z1, x1, b2, x2, rows_ref, parts, q_ref, zkin, tile_sums) = refs
    nx, ny = sz.grid_x, sz.grid_y
    here_x, here_y = lax.axis_index("dx"), lax.axis_index("dy")
    total = place_potential(sz, pots, psi, pot, tile_sums)
    energy = (jnp.sum(total) + jnp.sum(sums_ref[0:1, :])) / jnp.sum(sums_ref[1:2, :])
    energy_ref[0] = energy

    def residual(x0):
        for x in range(BLOCK):
            center = psi[x0 + x + 3, pl.ds(SUBLANES, ny), :]
            value = hpsi[x0 + x] + pot[x0 + x] * center - energy * spsi[x0 + x]
            res[x0 + x + 1, pl.ds(SUBLANES, ny), :] = value

    over_blocks(nx, residual)
    fill_rims(res, 1, nx, ny)
    restrict_into(nx, ny, 0, res, b1, rows_ref)
    restrict_into(nx // 2, ny // 2, 1, b1, b2, rows_ref)
    quarter_x, quarter_y = nx // 4, ny // 4
    x2[...] = level_numbers(2)[1] * b2[...]
    for _ in range(COARSE_SWEEPS):
        planes = []
        relax_rows(quarter_x, quarter_y, 2, x2, b2, lambda *piece: planes.append(piece))
        for x, y0, rows, value in planes:
            x2[x + 1, pl.ds(SUBLANES + y0, rows), :] = value
        fill_rims(x2, 1, quarter_x, quarter_y)
    coarse_two = lambda x, y: x2[x + 1, pl.ds(SUBLANES + y, SUBLANES), :]
    prolong_into(nx // 2, ny // 2, 1, coarse_two, b1, z1)

    def emit_one(x, y0, rows, value):
        x1[x, pl.ds(y0, rows), :] = value

    relax_rows(nx // 2, ny // 2, 1, z1, b1, emit_one)
    prolong_into(nx, ny, 0, lambda x, y: x1[x, pl.ds(y, SUBLANES), :], res, zfield)

    def emit_zero(x, y0, rows, value):
        direct[x + 3, pl.ds(SUBLANES + y0, rows), :] = value
        cells = pl.ds(pl.multiple_of(x * ny + y0, 16), rows)
        high, low = split(value)
        parts[cells, :LANES] = high
        parts[cells, LANES:] = low

    relax_rows(nx, ny, 0, zfield, res, emit_zero)
    fill_rims(direct, 3, nx, ny)
    zkin[...] = dot(parts[...], depth_matrix())
    active = active_columns(par_ref[2])
    columns = intersections(sz, w_ref, parts[...], wz_ref, active)
    q_ref[sz.factors :, LANES:] = jnp.zeros((sz.factors, LANES), jnp.bfloat16)
    matrix = par_ref[0] - energy * par_ref[1]
    projector_sources(sz, matrix, inner_lanes(columns), active, wz_ref, q_ref)

    def emit_change(at, rows, value):
        corr[at : at + rows, :] = value + zkin[at : at + rows, :]

    add_projectors(sz, a_ref, q_ref, emit_change)

    def line(index, carry):
        x0, (over, under) = index * BLOCK, carry
        for y0 in range(0, ny, SUBLANES):
            rows = pl.ds(y0, SUBLANES)
            for x, (center, value) in enumerate(planar_kinetic(direct, x0, y0, SUBLANES, BLOCK)):
                cells = pl.ds(pl.multiple_of((x0 + x) * ny + y0, SUBLANES), SUBLANES)
                value = value + (pot[x0 + x, rows, :] - energy) * center
                value = value + (1.0 / DEPTH_SCALE) * corr[cells, :]
                change[x0 + x, rows, :] = value
                over = over + value * res[x0 + x + 1, pl.ds(SUBLANES + y0, SUBLANES), :]
                under = under + value * value
        return over, under

    zero = jnp.zeros((SUBLANES, LANES), jnp.float32)
    over, under = lax.fori_loop(0, nx // BLOCK, line, (zero, zero))
    step = -jnp.sum(over) / jnp.sum(under)
    at_x, at_y = here_x * sz.tile_x, pl.multiple_of(here_y * sz.tile_y, 16)
    for x in range(sz.tile_x):
        cell = at_x + x
        inner = pl.ds(at_y + SUBLANES, sz.tile_y)
        bands_ref[0, x] = psi[cell + 3, inner, :] + step * direct[cell + 3, inner, :]
        resid_ref[0, x] = res[cell + 1, inner, :] + step * change[cell, pl.ds(at_y, sz.tile_y), :]


def partner(here, turn, count):
    return here ^ turn if count & (count - 1) == 0 else (here + turn) % count


def gathered(value, axis):
    count = lax.axis_size(axis)
    pairs = lambda turn: [(partner(i, turn, count), i) for i in range(count)]
    found = [value]
    for turn in range(1, count):
        found.append(lax.ppermute(value, axis, pairs(turn)))
    return found


def replicated(sz, wave_bands, potential, atom_offsets, proj_counts, dh_matrix, ds_matrix):
    vmem = pl.BlockSpec(memory_space=pltpu.VMEM)
    smem = pl.BlockSpec(memory_space=pltpu.SMEM)
    hbm = pl.BlockSpec(memory_space=pltpu.HBM)
    shape = lambda *dims: jax.ShapeDtypeStruct(dims, jnp.float32)
    half = lambda *dims: jax.ShapeDtypeStruct(dims, jnp.bfloat16)
    scratch = lambda *dims: pltpu.VMEM(dims, jnp.float32)
    grant = pltpu.CompilerParams(vmem_limit_bytes=VMEM_GRANT)
    cost = lambda flops: pl.CostEstimate(flops=flops, transcendentals=0, bytes_accessed=0)
    inputs = (
        wave_bands.reshape(sz.wave_rows, LANES),
        potential,
        atom_offsets.transpose(0, 3, 1, 2),
        proj_counts,
        dh_matrix.transpose(0, 1, 3, 2, 4),
        ds_matrix.transpose(0, 1, 3, 2, 4),
    )
    own = pl.pallas_call(
        functools.partial(pack_kernel, sz),
        out_shape=shape(sz.rows, LANES),
        in_specs=[hbm] * 6,
        out_specs=vmem,
        scratch_shapes=[
            scratch(*inputs[1].shape),
            pltpu.SMEM(inputs[2].shape, jnp.int32),
            pltpu.SMEM(inputs[3].shape, jnp.int32),
            scratch(*inputs[4].shape),
            scratch(*inputs[5].shape),
            pltpu.SemaphoreType.DMA((6,)),
        ],
        compiler_params=grant,
        name="pack",
    )(*(pltpu.with_memory_space_constraint(value, pltpu.HBM) for value in inputs))
    line = gathered(own, "dx")
    crossed = [gathered(block, "dy") for block in line]
    blocks = [each[turn] for turn in range(sz.tiles_y) for each in crossed]
    pieces = [block[sz.wave_rows : sz.wave_rows + sz.pot_rows] for block in line]
    chunks = jnp.concatenate(gathered(jnp.concatenate(pieces, axis=0), "band"), axis=0)
    pots = gathered(chunks, "dy")
    nx, ny = sz.grid_x, sz.grid_y
    padded = lambda x, y, width: (x + 2 * width, y + 2 * SUBLANES, LANES)
    q_scratch = pltpu.VMEM((2 * sz.factors, 2 * LANES), jnp.bfloat16)
    psi, spsi, zkin, inner, w, a, wz, par = pl.pallas_call(
        functools.partial(first_kernel, sz),
        out_shape=(
            shape(*padded(nx, ny, 3)),
            shape(nx, ny, LANES),
            shape(sz.cells, LANES),
            shape(sz.all_atoms, LANES),
            half(2 * sz.factors, sz.cells),
            half(sz.cells, 2 * sz.factors),
            shape(6, sz.all_atoms, LANES),
            shape(3, sz.all_atoms, LANES),
        ),
        in_specs=[vmem] * len(blocks),
        out_specs=(vmem,) * 8,
        scratch_shapes=[pltpu.VMEM((sz.cells, 2 * LANES), jnp.bfloat16), q_scratch]
        + [scratch(2 * sz.factors // LANES, n, LANES) for n in (nx, ny)],
        compiler_params=grant,
        cost_estimate=cost(3_000_000_000),
        name="first",
    )(*blocks)
    hpsi, sums = pl.pallas_call(
        functools.partial(second_kernel, sz),
        out_shape=(shape(nx, ny, LANES), shape(2, LANES)),
        in_specs=[vmem] * 7,
        out_specs=(vmem,) * 2,
        scratch_shapes=[q_scratch],
        compiler_params=grant,
        cost_estimate=cost(2_000_000_000),
        name="second",
    )(psi, spsi, zkin, inner, a, wz, par)
    made = (psi, hpsi, spsi, w, a, wz, par, sums)
    return pl.pallas_call(
        functools.partial(step_kernel, sz),
        out_shape=(
            jax.ShapeDtypeStruct(wave_bands.shape, jnp.float32),
            jax.ShapeDtypeStruct(wave_bands.shape, jnp.float32),
            shape(1),
        ),
        in_specs=[vmem] * (len(pots) + 8),
        out_specs=(vmem, vmem, smem),
        scratch_shapes=[
            scratch(nx, ny, LANES),
            scratch(sz.cells, LANES),
            scratch(*padded(nx, ny, 1)),
            scratch(*padded(nx, ny, 1)),
            scratch(*padded(nx, ny, 3)),
            scratch(nx, ny, LANES),
            scratch(*padded(nx // 2, ny // 2, 1)),
            scratch(*padded(nx // 2, ny // 2, 1)),
            scratch(nx // 2, ny // 2, LANES),
            scratch(*padded(nx // 4, ny // 4, 1)),
            scratch(*padded(nx // 4, ny // 4, 1)),
            scratch(ny // 2 // SUBLANES * (BLOCK // 2), 2 * SUBLANES, LANES),
            pltpu.VMEM((sz.cells, 2 * LANES), jnp.bfloat16),
            pltpu.VMEM((2 * sz.factors, 2 * LANES), jnp.bfloat16),
            scratch(sz.cells, LANES),
            scratch(sz.tiles_x * sz.tiles_y, sz.tile_y, LANES),
        ],
        compiler_params=grant,
        cost_estimate=cost(6_000_000_000),
        name="step",
    )(*pots, *made)


def on_device(wave_bands, potential, atom_offsets, proj_counts, dh_matrix, ds_matrix):
    sz = Sizes(
        wave_bands,
        potential,
        proj_counts.shape[2],
        lax.axis_size("dx"),
        lax.axis_size("dy"),
        lax.axis_size("band"),
    )
    step = functools.partial(replicated, sz) if sz.fits(VMEM_BUDGET) else distributed
    return step(wave_bands, potential, atom_offsets, proj_counts, dh_matrix, ds_matrix)


def solution(mesh):
    return jax.shard_map(
        on_device,
        mesh=mesh,
        in_specs=(
            P("band", "dx", "dy", None),
            P("dx", "dy", "band"),
            P("dx", "dy", None, None),
            P("dx", "dy", None),
            P("dx", "dy", None, None, None),
            P("dx", "dy", None, None, None),
        ),
        out_specs=(P("band", "dx", "dy", None), P("band", "dx", "dy", None), P("band")),
        check_vma=False,
    )
```

profile of v0, /device:TPU:0, one launch (start us, length us, event | category | flops | bytes accessed | tf_op | source)
XLA Modules:
  0.0 33.9 jit_solution(2738988260516306307)
XLA Ops:
  0.6 1.1 %pack.1.refs_0_ = f32[168,128]{1,0:T(8,128)S(1)} custom-call(f32[128,128]{1,0:T(8,128)} %bitcast.4, f32[8,16,32]{2,1,0:T(8,128)} %pot_ref.1, s32[1,3,1,4]{3,2,1,0:T(1,128)} %bitcast.7, s32[1,1,4]{2,1,0:T(1,128)} %counts_ref.1, f32[1,1,9,4,9]{4,3,2,1,0:T(4,128)} %bitcast.5, f32[1,1,9,4,9]{4,3,2,1,0:T(4,128)} %bitcast.6), custom_call_target="tpu_custom_call" | custom-call | tf_op jit(solution)/shard_map/pack/pallas_call | solution.py:865
  1.7 5.1 %collective-permute-start.2 = (f32[168,128]{1,0:T(8,128)S(1)}, f32[168,128]{1,0:T(8,128)S(1)}, u32[]{:S(2)}, u32[]{:S(2)}) collective-permute-start(f32[168,128]{1,0:T(8,128)S(1)} %pack.1.refs_0_), channel_id=1, source_target_pairs={{6,0},{4,2},{2,4},{0,6},{7,1},{5,3},{3,5},{1,7},{14,8},{12,10},{10... | collective-permute-start | bytes 258056 | tf_op jit(solution)/shard_map/ppermute | solution.py:844
  6.9 0.0 collective-permute-start
  6.9 0.6 %collective-permute-start.1 = (f32[168,128]{1,0:T(8,128)S(1)}, f32[168,128]{1,0:T(8,128)S(1)}, u32[]{:S(2)}, u32[]{:S(2)}) collective-permute-start(f32[168,128]{1,0:T(8,128)S(1)} %pack.1.refs_0_), channel_id=1, source_target_pairs={{4,0},{6,2},{0,4},{2,6},{5,1},{7,3},{1,5},{3,7},{12,8},{14,10},{8,... | collective-permute-start | bytes 258056 | tf_op jit(solution)/shard_map/ppermute | solution.py:844
  7.5 5.5 %collective-permute-done.refs_1_ = f32[168,128]{1,0:T(8,128)S(1)} collective-permute-done((f32[168,128]{1,0:T(8,128)S(1)}, f32[168,128]{1,0:T(8,128)S(1)}, u32[]{:S(2)}, u32[]{:S(2)}) %collective-permute-start) | collective-permute-done | bytes 86048 | tf_op jit(solution)/shard_map/ppermute | solution.py:844
  13.1 1.0 %collective-permute-done.1.refs_2_ = f32[168,128]{1,0:T(8,128)S(1)} collective-permute-done((f32[168,128]{1,0:T(8,128)S(1)}, f32[168,128]{1,0:T(8,128)S(1)}, u32[]{:S(2)}, u32[]{:S(2)}) %collective-permute-start.1) | collective-permute-done | bytes 86048 | tf_op jit(solution)/shard_map/ppermute | solution.py:844
  14.1 0.0 collective-permute-done.2.refs_3_
  14.1 1.6 %collective-permute-start.3 = (f32[128,128]{1,0:T(8,128)S(1)}, f32[128,128]{1,0:T(8,128)S(1)}, u32[]{:S(2)}, u32[]{:S(2)}) collective-permute-start(f32[128,128]{1,0:T(8,128)S(1)} %pad_maximum_fusion), channel_id=1, source_target_pairs={{8,0},{0,8},{24,16},{16,24},{9,1},{1,9},{25,17},{17,25},{10,2},{2,... | collective-permute-start | bytes 196616 | tf_op jit(solution)/shard_map/ppermute | solution.py:844
  15.7 0.0 collective-permute-start.7
  15.7 1.5 %collective-permute-start.4 = (f32[128,128]{1,0:T(8,128)S(1)}, f32[128,128]{1,0:T(8,128)S(1)}, u32[]{:S(2)}, u32[]{:S(2)}) collective-permute-start(f32[128,128]{1,0:T(8,128)S(1)} %pad_maximum_fusion), channel_id=1, source_target_pairs={{16,0},{24,8},{0,16},{8,24},{17,1},{25,9},{1,17},{9,25},{18,2},{26... | collective-permute-start | bytes 196616 | tf_op jit(solution)/shard_map/ppermute | solution.py:844
  17.2 0.5 %collective-permute-start.5 = (f32[128,128]{1,0:T(8,128)S(1)}, f32[128,128]{1,0:T(8,128)S(1)}, u32[]{:S(2)}, u32[]{:S(2)}) collective-permute-start(f32[128,128]{1,0:T(8,128)S(1)} %pad_maximum_fusion), channel_id=1, source_target_pairs={{24,0},{16,8},{8,16},{0,24},{25,1},{17,9},{9,17},{1,25},{26,2},{18... | collective-permute-start | bytes 196616 | tf_op jit(solution)/shard_map/ppermute | solution.py:844
  17.7 0.0 collective-permute-start.10
  17.7 0.8 %collective-permute-done.3 = f32[128,128]{1,0:T(8,128)S(1)} collective-permute-done((f32[128,128]{1,0:T(8,128)S(1)}, f32[128,128]{1,0:T(8,128)S(1)}, u32[]{:S(2)}, u32[]{:S(2)}) %collective-permute-start.3) | collective-permute-done | bytes 65568 | tf_op jit(solution)/shard_map/ppermute | solution.py:844
  18.5 0.0 collective-permute-start.8
  18.5 1.7 %collective-permute-done.4 = f32[128,128]{1,0:T(8,128)S(1)} collective-permute-done((f32[128,128]{1,0:T(8,128)S(1)}, f32[128,128]{1,0:T(8,128)S(1)}, u32[]{:S(2)}, u32[]{:S(2)}) %collective-permute-start.4) | collective-permute-done | bytes 65568 | tf_op jit(solution)/shard_map/ppermute | solution.py:844
  20.2 0.0 collective-permute-start.9
  20.2 2.2 %collective-permute-done.5 = f32[128,128]{1,0:T(8,128)S(1)} collective-permute-done((f32[128,128]{1,0:T(8,128)S(1)}, f32[128,128]{1,0:T(8,128)S(1)}, u32[]{:S(2)}, u32[]{:S(2)}) %collective-permute-start.5) | collective-permute-done | bytes 65568 | tf_op jit(solution)/shard_map/ppermute | solution.py:844
  22.4 0.0 collective-permute-start.6
  22.4 0.0 collective-permute-done.7.refs_4_
  22.4 0.0 collective-permute-done.10.refs_7_
  22.4 0.0 collective-permute-done.8.refs_5_
  22.4 0.0 collective-permute-done.9.refs_6_
  22.4 3.7 %first.1 = (f32[38,48,128]{2,1,0:T(8,128)S(1)}, f32[32,32,128]{2,1,0:T(8,128)S(1)}, f32[1024,128]{1,0:T(8,128)S(1)}, f32[32,128]{1,0:T(8,128)S(1)}, bf16[640,102...) custom-call(f32[168,128]{1,0:T(8,128)S(1)} %pack.1.refs_0_, ...), custom_call_target="tpu_custom_call" | custom-call | flops 3000000000 | tf_op jit(solution)/shard_map/first/pallas_call | solution.py:890
  26.2 1.2 %second.1 = (f32[32,32,128]{2,1,0:T(8,128)S(1)}, f32[2,128]{1,0:T(2,128)S(1)}) custom-call(f32[38,48,128]{2,1,0:T(8,128)S(1)} %get-tuple-element.13.refs_0_.refs_2_, f32[32,32,128]{2,1,0:T(8,128)S(1)} %get-tuple-element.14.refs_1_.refs_4_, f32[1024,128]{1,0:T(8,128)S(1)} %get-tuple-element.15.refs_2_, f32[32,128]{1,0:T(8,128)S(1)} %get-tuple-element.16.refs_3_, ...), custom_call_target="tpu_custom_call" | custom-call | flops 2000000000 | tf_op jit(solution)/shard_map/second/pallas_call | solution.py:910
  27.4 0.0 collective-permute-done.6.refs_1_
  27.4 6.5 %step.1 = (f32[1,8,16,128]{3,2,1,0:T(8,128)}, f32[1,8,16,128]{3,2,1,0:T(8,128)}, f32[1]{0:T(128)}) custom-call(f32[512,128]{1,0:T(8,128)S(1)} %constant_dynamic-update-slice_fusion.refs_0_, f32[512,128]{1,0:T(8,128)S(1)} %collective-permute-done.6.refs_1_, f32[38,48,128]{2,1,0:T(8,128)S(1)} %get-tuple-element.13.refs_0_.refs_2_, ...), custom_call_target="tpu_custom_call" | custom-call | flops 6000000000 | tf_op jit(solution)/shard_map/step/pallas_call | solution.py:921
  (8 shorter events, 0.0 us)
Async XLA Ops:
  1.7 12.4 %collective-permute-start.2 = (f32[168,128]{1,0:T(8,128)S(1)}, f32[168,128]{1,0:T(8,128)S(1)}, u32[]{:S(2)}, u32[]{:S(2)}) collective-permute-start(f32[168,128]{1,0:T(8,128)S(1)} %pack.1.refs_0_), channel_id=1, source_target_pairs={{6,0},{4,2},{2,4},{0,6},{7,1},{5,3},{3,5},{1,7},{14,8},{12,10},{10... | collective-permute-start | bytes 258056 | tf_op jit(solution)/shard_map/ppermute | solution.py:844
  6.9 6.2 %collective-permute-start = (f32[168,128]{1,0:T(8,128)S(1)}, f32[168,128]{1,0:T(8,128)S(1)}, u32[]{:S(2)}, u32[]{:S(2)}) collective-permute-start(f32[168,128]{1,0:T(8,128)S(1)} %pack.1.refs_0_), channel_id=1, source_target_pairs={{2,0},{0,2},{6,4},{4,6},{3,1},{1,3},{7,5},{5,7},{10,8},{8,10},{14,... | collective-permute-start | bytes 258056 | tf_op jit(solution)/shard_map/ppermute | solution.py:844
  6.9 7.2 %collective-permute-start.1 = (f32[168,128]{1,0:T(8,128)S(1)}, f32[168,128]{1,0:T(8,128)S(1)}, u32[]{:S(2)}, u32[]{:S(2)}) collective-permute-start(f32[168,128]{1,0:T(8,128)S(1)} %pack.1.refs_0_), channel_id=1, source_target_pairs={{4,0},{6,2},{0,4},{2,6},{5,1},{7,3},{1,5},{3,7},{12,8},{14,10},{8,... | collective-permute-start | bytes 258056 | tf_op jit(solution)/shard_map/ppermute | solution.py:844
  14.1 4.3 %collective-permute-start.3 = (f32[128,128]{1,0:T(8,128)S(1)}, f32[128,128]{1,0:T(8,128)S(1)}, u32[]{:S(2)}, u32[]{:S(2)}) collective-permute-start(f32[128,128]{1,0:T(8,128)S(1)} %pad_maximum_fusion), channel_id=1, source_target_pairs={{8,0},{0,8},{24,16},{16,24},{9,1},{1,9},{25,17},{17,25},{10,2},{2,... | collective-permute-start | bytes 196616 | tf_op jit(solution)/shard_map/ppermute | solution.py:844
  15.7 6.7 %collective-permute-start.7 = (f32[168,128]{1,0:T(8,128)S(1)}, f32[168,128]{1,0:T(8,128)S(1)}, u32[]{:S(2)}, u32[]{:S(2)}) collective-permute-start(f32[168,128]{1,0:T(8,128)S(1)} %pack.1.refs_0_), channel_id=1, source_target_pairs={{1,0},{0,1},{3,2},{2,3},{5,4},{4,5},{7,6},{6,7},{9,8},{8,9},{11,10... | collective-permute-start | bytes 258056 | tf_op jit(solution)/shard_map/ppermute | solution.py:844
  15.7 4.5 %collective-permute-start.4 = (f32[128,128]{1,0:T(8,128)S(1)}, f32[128,128]{1,0:T(8,128)S(1)}, u32[]{:S(2)}, u32[]{:S(2)}) collective-permute-start(f32[128,128]{1,0:T(8,128)S(1)} %pad_maximum_fusion), channel_id=1, source_target_pairs={{16,0},{24,8},{0,16},{8,24},{17,1},{25,9},{1,17},{9,25},{18,2},{26... | collective-permute-start | bytes 196616 | tf_op jit(solution)/shard_map/ppermute | solution.py:844
  17.2 5.2 %collective-permute-start.5 = (f32[128,128]{1,0:T(8,128)S(1)}, f32[128,128]{1,0:T(8,128)S(1)}, u32[]{:S(2)}, u32[]{:S(2)}) collective-permute-start(f32[128,128]{1,0:T(8,128)S(1)} %pad_maximum_fusion), channel_id=1, source_target_pairs={{24,0},{16,8},{8,16},{0,24},{25,1},{17,9},{9,17},{1,25},{26,2},{18... | collective-permute-start | bytes 196616 | tf_op jit(solution)/shard_map/ppermute | solution.py:844
  17.7 4.7 %collective-permute-start.10 = (f32[168,128]{1,0:T(8,128)S(1)}, f32[168,128]{1,0:T(8,128)S(1)}, u32[]{:S(2)}, u32[]{:S(2)}) collective-permute-start(f32[168,128]{1,0:T(8,128)S(1)} %collective-permute-done.2.refs_3_), channel_id=1, source_target_pairs={{1,0},{0,1},{3,2},{2,3},{5,4},{4,5},{7,6},{6,7},{9,8},{8,9},{11,10... | collective-permute-start | bytes 258056 | tf_op jit(solution)/shard_map/ppermute | solution.py:844
  18.5 4.0 %collective-permute-start.8 = (f32[168,128]{1,0:T(8,128)S(1)}, f32[168,128]{1,0:T(8,128)S(1)}, u32[]{:S(2)}, u32[]{:S(2)}) collective-permute-start(f32[168,128]{1,0:T(8,128)S(1)} %collective-permute-done.refs_1_), channel_id=1, source_target_pairs={{1,0},{0,1},{3,2},{2,3},{5,4},{4,5},{7,6},{6,7},{9,8},{8,9},{11,10... | collective-permute-start | bytes 258056 | tf_op jit(solution)/shard_map/ppermute | solution.py:844
  20.2 2.2 %collective-permute-start.9 = (f32[168,128]{1,0:T(8,128)S(1)}, f32[168,128]{1,0:T(8,128)S(1)}, u32[]{:S(2)}, u32[]{:S(2)}) collective-permute-start(f32[168,128]{1,0:T(8,128)S(1)} %collective-permute-done.1.refs_2_), channel_id=1, source_target_pairs={{1,0},{0,1},{3,2},{2,3},{5,4},{4,5},{7,6},{6,7},{9,8},{8,9},{11,10... | collective-permute-start | bytes 258056 | tf_op jit(solution)/shard_map/ppermute | solution.py:844
  22.4 5.0 %collective-permute-start.6 = (f32[512,128]{1,0:T(8,128)S(1)}, f32[512,128]{1,0:T(8,128)S(1)}, u32[]{:S(2)}, u32[]{:S(2)}) collective-permute-start(f32[512,128]{1,0:T(8,128)S(1)} %constant_dynamic-update-slice_fusion.refs_0_), channel_id=1, source_target_pairs={{1,0},{0,1},{3,2},{2,3},{5,4},{4,5},{7,6},{6,7},{9,8},{8,9},{11,10... | collective-permute-start | bytes 786440 | tf_op jit(solution)/shard_map/ppermute | solution.py:844
where the time goes:
time: 34 us; the launch traced here: 33.9 us
  Pallas kernels  12.5 us (37%)
  waiting for transfers between devices  11.2 us (33%)
  starting transfers between devices  9.35 us (28%)
  between operations  0.72 us (2%)
    ppermute x11, waiting for transfers between devices, gathered(): found.append(lax.ppermute(value, axis, pairs(turn)))  11.2 us
    ppermute x11, starting transfers between devices, gathered(): found.append(lax.ppermute(value, axis, pairs(turn)))  9.35 us
    pallas_call x1, Pallas kernels, replicated(): pl.pallas_call(functools.partial(step_kernel, sz), out_shape=(jax.ShapeDt...  6.48 us
    pallas_call x1, Pallas kernels, replicated(): pl.pallas_call(functools.partial(first_kernel, sz), out_shape=(shape(*pad...  3.71 us
    pallas_call x1, Pallas kernels, replicated(): pl.pallas_call(functools.partial(second_kernel, sz), out_shape=(shape(nx,...  1.22 us
    pallas_call x1, Pallas kernels, replicated(): pl.pallas_call(functools.partial(pack_kernel, sz), out_shape=shape(sz.row...  1.11 us
  transfers between devices with their start and end apart: 11, of which 5 were waited for; matrix products, arithmetic and copies ran while one was open for 0% of the time, Pallas kernels for 15%

commit v1 on v0

--- a/solution.py
+++ b/solution.py
@@ -417,16 +417,8 @@
 
 
 def over_blocks(count, body):
-    if count <= 2 * BLOCK:
-        for x0 in range(0, count, BLOCK):
-            body(x0)
-        return
-
-    def step(index, carry):
-        body(index * BLOCK)
-        return carry
-
-    lax.fori_loop(0, count // BLOCK, step, 0)
+    for x0 in range(0, count, BLOCK):
+        body(x0)
 
 
 def plane_weights(sz, meta, w_ref, a_ref, wx_ref, wy_ref):
@@ -501,10 +493,14 @@
     wz_ref[5] = radial[2] * (offset * offset)
 
 
-def intersections(sz, w_ref, parts, wz_ref, active):
-    high, low = parts[:, :LANES], parts[:, LANES:]
-    sums = dot(w_ref[: sz.factors], high)
-    sums = sums + (dot(w_ref[: sz.factors], low) + dot(w_ref[sz.factors :], high))
+def plane_sums(sz, w_ref, parts, x0):
+    cells = slice(x0 * sz.grid_y, (x0 + BLOCK) * sz.grid_y)
+    field = parts[cells, :]
+    sums = dot(w_ref[:, cells], field)
+    return halves(sums[: sz.factors]) + sums[sz.factors :, :LANES]
+
+
+def intersections(sz, sums, wz_ref, active):
     u = [sums[c * sz.all_atoms : (c + 1) * sz.all_atoms] for c in range(len(PLANE_FACTORS))]
     products = [
         u[0] * wz_ref[0],
@@ -576,8 +572,7 @@
 
 def first_kernel(sz, *refs):
     blocks, refs = refs[: sz.tiles_x * sz.tiles_y], refs[sz.tiles_x * sz.tiles_y :]
-    (psi, spsi, zkin, inner_ref, w_ref, a_ref, wz_ref, par_ref), refs = refs[:8], refs[8:]
-    (parts, q_ref, wx_ref, wy_ref) = refs
+    (psi, zkin, inner_ref, w_ref, a_ref, wz_ref, par_ref, parts, wx_ref, wy_ref) = refs
     nx, ny = sz.grid_x, sz.grid_y
     for index, block in enumerate(blocks):
         tile_x, tile_y = tile_at(sz, index)
@@ -604,12 +599,22 @@
     depth_weights(meta, wz_ref)
     plane_weights(sz, meta, w_ref, a_ref, wx_ref, wy_ref)
     active = active_columns(meta)
-    columns = intersections(sz, w_ref, parts[...], wz_ref, active)
+    sums = None
+    for x0 in range(0, nx, BLOCK):
+        term = plane_sums(sz, w_ref, parts, x0)
+        sums = term if sums is None else sums + term
+    columns = intersections(sz, sums, wz_ref, active)
     zkin[...] = dot(parts[...], depth_matrix())
     inner = inner_lanes(columns)
     inner_ref[...] = inner
+
+
+def second_kernel(sz, *refs):
+    (psi, zkin, inner_ref, a_ref, wz_ref, par_ref, hpsi, spsi, sums_ref, q_ref) = refs
+    nx, ny = sz.grid_x, sz.grid_y
     q_ref[sz.factors :, LANES:] = jnp.zeros((sz.factors, LANES), jnp.bfloat16)
-    projector_sources(sz, par_ref[1], inner, active, wz_ref, q_ref)
+    active = active_columns(par_ref[2])
+    projector_sources(sz, par_ref[1], inner_ref[...], active, wz_ref, q_ref)
 
     def emit_s(at, rows, value):
         x0, count = at // ny, rows // ny
@@ -617,37 +622,30 @@
         spsi[x0 : x0 + count] = center + (1.0 / DEPTH_SCALE) * value.reshape(count, ny, LANES)
 
     add_projectors(sz, a_ref, q_ref, emit_s)
-
-
-def second_kernel(sz, *refs):
-    (psi, spsi, zkin, inner_ref, a_ref, wz_ref, par_ref, hpsi, sums_ref, q_ref) = refs
-    nx, ny = sz.grid_x, sz.grid_y
-    q_ref[sz.factors :, LANES:] = jnp.zeros((sz.factors, LANES), jnp.bfloat16)
-    active = active_columns(par_ref[2])
     projector_sources(sz, par_ref[0], inner_ref[...], active, wz_ref, q_ref)
+    for x0 in range(0, nx, BLOCK):
+        for y0 in range(0, ny, SUBLANES):
+            for x, (_, value) in enumerate(planar_kinetic(psi, x0, y0, SUBLANES, BLOCK)):
+                hpsi[x0 + x, y0 : y0 + SUBLANES, :] = value
+    found = []
 
     def emit_h(at, rows, value):
-        x0, count = at // ny, rows // ny
-        total = value + zkin[at : at + rows, :]
-        hpsi[x0 : x0 + count] = (1.0 / DEPTH_SCALE) * total.reshape(count, ny, LANES)
+        planes = slice(at // ny, (at + rows) // ny)
+        shape = (rows // ny, ny, LANES)
+        center = psi[at // ny + 3 : (at + rows) // ny + 3, SUBLANES : SUBLANES + ny, :]
+        value = (1.0 / DEPTH_SCALE) * (value + zkin[at : at + rows, :]).reshape(shape)
+        value = value + hpsi[planes]
+        hpsi[planes] = value
+        found.append((folded(value * center), folded(spsi[planes] * center)))
 
     add_projectors(sz, a_ref, q_ref, emit_h)
-
-    def block(index, carry):
-        x0, (energy, norm) = index * BLOCK, carry
-        for y0 in range(0, ny, SUBLANES):
-            rows = pl.ds(y0, SUBLANES)
-            for x, (center, value) in enumerate(planar_kinetic(psi, x0, y0, SUBLANES, BLOCK)):
-                value = value + hpsi[x0 + x, rows, :]
-                hpsi[x0 + x, rows, :] = value
-                energy = energy + value * center
-                norm = norm + spsi[x0 + x, rows, :] * center
-        return energy, norm
-
-    zero = jnp.zeros((SUBLANES, LANES), jnp.float32)
-    energy, norm = lax.fori_loop(0, nx // BLOCK, block, (zero, zero))
-    sums_ref[0:1, :] = jnp.sum(energy, axis=0, keepdims=True)
-    sums_ref[1:2, :] = jnp.sum(norm, axis=0, keepdims=True)
+    for row in range(2):
+        total = found[0][row] + found[1][row]
+        sums_ref[row : row + 1, :] = jnp.sum(total, axis=0, keepdims=True)
+
+
+def folded(value):
+    return jnp.sum(value.reshape(-1, SUBLANES, LANES), axis=0)
 
 
 def pair_lanes(value, step):
@@ -685,7 +683,7 @@
     fill_rims(target, 1, count_x // 2, count_y // 2)
 
 
-def relax_rows(count_x, count_y, level, guess_ref, source, emit):
+def relax_rows(count_x, count_y, level, guess_ref, source, emit, after_block=lambda x0: None):
     spread, guess = level_numbers(level)
     rows = min(2 * SUBLANES, count_y)
 
@@ -696,6 +694,7 @@
                 right = source[x0 + x + 1, pl.ds(SUBLANES + y0, rows), :]
                 value = (1.0 - RELAXATION) * center + guess * right + (guess * spread) * around
                 emit(x0 + x, y0, rows, value)
+        after_block(x0)
 
     over_blocks(count_x, body)
 
@@ -753,7 +752,7 @@
     pots, refs = refs[: sz.tiles_y], refs[sz.tiles_y :]
     (psi, hpsi, spsi, w_ref, a_ref, wz_ref, par_ref, sums_ref), refs = refs[:8], refs[8:]
     (bands_ref, resid_ref, energy_ref), refs = refs[:3], refs[3:]
-    (pot, corr, res, zfield, direct, change, b1, z1, x1, b2, x2, rows_ref, parts, q_ref, zkin, tile_sums) = refs
+    (pot, res, zfield, direct, change, b1, z1, x1, b2, x2, rows_ref, parts, q_ref, zkin, tile_sums) = refs
     nx, ny = sz.grid_x, sz.grid_y
     here_x, here_y = lax.axis_index("dx"), lax.axis_index("dy")
     total = place_potential(sz, pots, psi, pot, tile_sums)
@@ -789,40 +788,44 @@
 
     def emit_zero(x, y0, rows, value):
         direct[x + 3, pl.ds(SUBLANES + y0, rows), :] = value
-        cells = pl.ds(pl.multiple_of(x * ny + y0, 16), rows)
+        cells = slice(x * ny + y0, x * ny + y0 + rows)
         high, low = split(value)
         parts[cells, :LANES] = high
         parts[cells, LANES:] = low
 
-    relax_rows(nx, ny, 0, zfield, res, emit_zero)
+    found = []
+
+    def after_block(x0):
+        cells = slice(x0 * ny, (x0 + BLOCK) * ny)
+        zkin[cells, :] = dot(parts[cells, :], depth_matrix())
+        term = plane_sums(sz, w_ref, parts, x0)
+        found.append(term if not found else found[-1] + term)
+
+    relax_rows(nx, ny, 0, zfield, res, emit_zero, after_block)
     fill_rims(direct, 3, nx, ny)
-    zkin[...] = dot(parts[...], depth_matrix())
     active = active_columns(par_ref[2])
-    columns = intersections(sz, w_ref, parts[...], wz_ref, active)
+    columns = intersections(sz, found[-1], wz_ref, active)
+    for x0 in range(0, nx, BLOCK):
+        for y0 in range(0, ny, SUBLANES):
+            for x, (center, value) in enumerate(planar_kinetic(direct, x0, y0, SUBLANES, BLOCK)):
+                rows = slice(y0, y0 + SUBLANES)
+                change[x0 + x, rows, :] = value + (pot[x0 + x, rows, :] - energy) * center
     q_ref[sz.factors :, LANES:] = jnp.zeros((sz.factors, LANES), jnp.bfloat16)
     matrix = par_ref[0] - energy * par_ref[1]
     projector_sources(sz, matrix, inner_lanes(columns), active, wz_ref, q_ref)
+    found = []
 
     def emit_change(at, rows, value):
-        corr[at : at + rows, :] = value + zkin[at : at + rows, :]
+        planes = slice(at // ny, (at + rows) // ny)
+        shape = (rows // ny, ny, LANES)
+        value = (1.0 / DEPTH_SCALE) * (value + zkin[at : at + rows, :]).reshape(shape)
+        value = value + change[planes]
+        change[planes] = value
+        before = res[at // ny + 1 : (at + rows) // ny + 1, SUBLANES : SUBLANES + ny, :]
+        found.append((folded(value * before), folded(value * value)))
 
     add_projectors(sz, a_ref, q_ref, emit_change)
-
-    def line(index, carry):
-        x0, (over, under) = index * BLOCK, carry
-        for y0 in range(0, ny, SUBLANES):
-            rows = pl.ds(y0, SUBLANES)
-            for x, (center, value) in enumerate(planar_kinetic(direct, x0, y0, SUBLANES, BLOCK)):
-                cells = pl.ds(pl.multiple_of((x0 + x) * ny + y0, SUBLANES), SUBLANES)
-                value = value + (pot[x0 + x, rows, :] - energy) * center
-                value = value + (1.0 / DEPTH_SCALE) * corr[cells, :]
-                change[x0 + x, rows, :] = value
-                over = over + value * res[x0 + x + 1, pl.ds(SUBLANES + y0, SUBLANES), :]
-                under = under + value * value
-        return over, under
-
-    zero = jnp.zeros((SUBLANES, LANES), jnp.float32)
-    over, under = lax.fori_loop(0, nx // BLOCK, line, (zero, zero))
+    over, under = (found[0][k] + found[1][k] for k in range(2))
     step = -jnp.sum(over) / jnp.sum(under)
     at_x, at_y = here_x * sz.tile_x, pl.multiple_of(here_y * sz.tile_y, 16)
     for x in range(sz.tile_x):
@@ -887,11 +890,10 @@
     nx, ny = sz.grid_x, sz.grid_y
     padded = lambda x, y, width: (x + 2 * width, y + 2 * SUBLANES, LANES)
     q_scratch = pltpu.VMEM((2 * sz.factors, 2 * LANES), jnp.bfloat16)
-    psi, spsi, zkin, inner, w, a, wz, par = pl.pallas_call(
+    psi, zkin, inner, w, a, wz, par = pl.pallas_call(
         functools.partial(first_kernel, sz),
         out_shape=(
             shape(*padded(nx, ny, 3)),
-            shape(nx, ny, LANES),
             shape(sz.cells, LANES),
             shape(sz.all_atoms, LANES),
             half(2 * sz.factors, sz.cells),
@@ -900,23 +902,23 @@
             shape(3, sz.all_atoms, LANES),
         ),
         in_specs=[vmem] * len(blocks),
-        out_specs=(vmem,) * 8,
-        scratch_shapes=[pltpu.VMEM((sz.cells, 2 * LANES), jnp.bfloat16), q_scratch]
+        out_specs=(vmem,) * 7,
+        scratch_shapes=[pltpu.VMEM((sz.cells, 2 * LANES), jnp.bfloat16)]
         + [scratch(2 * sz.factors // LANES, n, LANES) for n in (nx, ny)],
         compiler_params=grant,
         cost_estimate=cost(3_000_000_000),
         name="first",
     )(*blocks)
-    hpsi, sums = pl.pallas_call(
+    hpsi, spsi, sums = pl.pallas_call(
         functools.partial(second_kernel, sz),
-        out_shape=(shape(nx, ny, LANES), shape(2, LANES)),
-        in_specs=[vmem] * 7,
-        out_specs=(vmem,) * 2,
+        out_shape=(shape(nx, ny, LANES), shape(nx, ny, LANES), shape(2, LANES)),
+        in_specs=[vmem] * 6,
+        out_specs=(vmem,) * 3,
         scratch_shapes=[q_scratch],
         compiler_params=grant,
         cost_estimate=cost(2_000_000_000),
         name="second",
-    )(psi, spsi, zkin, inner, a, wz, par)
+    )(psi, zkin, inner, a, wz, par)
     made = (psi, hpsi, spsi, w, a, wz, par, sums)
     return pl.pallas_call(
         functools.partial(step_kernel, sz),
@@ -929,7 +931,6 @@
         out_specs=(vmem, vmem, smem),
         scratch_shapes=[
             scratch(nx, ny, LANES),
-            scratch(sz.cells, LANES),
             scratch(*padded(nx, ny, 1)),
             scratch(*padded(nx, ny, 1)),
             scratch(*padded(nx, ny, 3)),

time: 34 us -> 30.7 us (0.903)
  Pallas kernels: 12.5 us -> 9.22 us
    pallas_call x1, Pallas kernels: 6.48 us -> 4.49 us  [replicated(): pl.pallas_call(functools.partial(step_kernel, sz), out_shape=(jax.ShapeDt...]
    pallas_call x1, Pallas kernels: 3.71 us -> 2.08 us  [replicated(): pl.pallas_call(functools.partial(first_kernel, sz), out_shape=(shape(*pad...]
  transfers between devices with their start and end apart: 11 -> 11, of which waited for: 5 -> 5; matrix products, arithmetic and copies ran while one was open for 0% -> 0% of each run, Pallas kernels for 15% -> 12%
where the time goes in v1:
time: 30.7 us; the launch traced here: 30.6 us
  waiting for transfers between devices  11.2 us (36%)
  starting transfers between devices  9.35 us (30%)
  Pallas kernels  9.22 us (30%)
  between operations  0.72 us (2%)
    ppermute x11, waiting for transfers between devices, gathered(): found.append(lax.ppermute(value, axis, pairs(turn)))  11.2 us
    ppermute x11, starting transfers between devices, gathered(): found.append(lax.ppermute(value, axis, pairs(turn)))  9.35 us
    pallas_call x1, Pallas kernels, replicated(): pl.pallas_call(functools.partial(step_kernel, sz), out_shape=(jax.ShapeDt...  4.49 us
    pallas_call x1, Pallas kernels, replicated(): pl.pallas_call(functools.partial(first_kernel, sz), out_shape=(shape(*pad...  2.08 us
    pallas_call x1, Pallas kernels, replicated(): pl.pallas_call(functools.partial(second_kernel, sz), out_shape=(shape(nx,...  1.54 us
    pallas_call x1, Pallas kernels, replicated(): pl.pallas_call(functools.partial(pack_kernel, sz), out_shape=shape(sz.row...  1.11 us
  transfers between devices with their start and end apart: 11, of which 5 were waited for; matrix products, arithmetic and copies ran while one was open for 0% of the time, Pallas kernels for 12%

profile of v1, /device:TPU:0, one launch (start us, length us, event | category | flops | bytes accessed | tf_op | source)
XLA Modules:
  0.0 30.6 jit_solution(17644303544752521128)
XLA Ops:
  0.6 1.1 %pack.1.refs_0_ = f32[168,128]{1,0:T(8,128)S(1)} custom-call(f32[128,128]{1,0:T(8,128)} %bitcast.4, f32[8,16,32]{2,1,0:T(8,128)} %pot_ref.1, s32[1,3,1,4]{3,2,1,0:T(1,128)} %bitcast.7, s32[1,1,4]{2,1,0:T(1,128)} %counts_ref.1, f32[1,1,9,4,9]{4,3,2,1,0:T(4,128)} %bitcast.5, f32[1,1,9,4,9]{4,3,2,1,0:T(4,128)} %bitcast.6), custom_call_target="tpu_custom_call" | custom-call | tf_op jit(solution)/shard_map/pack/pallas_call | solution.py:868
  1.7 5.1 %collective-permute-start.2 = (f32[168,128]{1,0:T(8,128)S(1)}, f32[168,128]{1,0:T(8,128)S(1)}, u32[]{:S(2)}, u32[]{:S(2)}) collective-permute-start(f32[168,128]{1,0:T(8,128)S(1)} %pack.1.refs_0_), channel_id=1, source_target_pairs={{6,0},{4,2},{2,4},{0,6},{7,1},{5,3},{3,5},{1,7},{14,8},{12,10},{10... | collective-permute-start | bytes 258056 | tf_op jit(solution)/shard_map/ppermute | solution.py:847
  6.9 0.0 collective-permute-start
  6.9 0.6 %collective-permute-start.1 = (f32[168,128]{1,0:T(8,128)S(1)}, f32[168,128]{1,0:T(8,128)S(1)}, u32[]{:S(2)}, u32[]{:S(2)}) collective-permute-start(f32[168,128]{1,0:T(8,128)S(1)} %pack.1.refs_0_), channel_id=1, source_target_pairs={{4,0},{6,2},{0,4},{2,6},{5,1},{7,3},{1,5},{3,7},{12,8},{14,10},{8,... | collective-permute-start | bytes 258056 | tf_op jit(solution)/shard_map/ppermute | solution.py:847
  7.5 5.5 %collective-permute-done.refs_1_ = f32[168,128]{1,0:T(8,128)S(1)} collective-permute-done((f32[168,128]{1,0:T(8,128)S(1)}, f32[168,128]{1,0:T(8,128)S(1)}, u32[]{:S(2)}, u32[]{:S(2)}) %collective-permute-start) | collective-permute-done | bytes 86048 | tf_op jit(solution)/shard_map/ppermute | solution.py:847
  13.1 1.0 %collective-permute-done.1.refs_2_ = f32[168,128]{1,0:T(8,128)S(1)} collective-permute-done((f32[168,128]{1,0:T(8,128)S(1)}, f32[168,128]{1,0:T(8,128)S(1)}, u32[]{:S(2)}, u32[]{:S(2)}) %collective-permute-start.1) | collective-permute-done | bytes 86048 | tf_op jit(solution)/shard_map/ppermute | solution.py:847
  14.1 0.0 collective-permute-done.2.refs_3_
  14.1 1.6 %collective-permute-start.3 = (f32[128,128]{1,0:T(8,128)S(1)}, f32[128,128]{1,0:T(8,128)S(1)}, u32[]{:S(2)}, u32[]{:S(2)}) collective-permute-start(f32[128,128]{1,0:T(8,128)S(1)} %pad_maximum_fusion), channel_id=1, source_target_pairs={{8,0},{0,8},{24,16},{16,24},{9,1},{1,9},{25,17},{17,25},{10,2},{2,... | collective-permute-start | bytes 196616 | tf_op jit(solution)/shard_map/ppermute | solution.py:847
  15.7 0.0 collective-permute-start.7
  15.7 1.5 %collective-permute-start.4 = (f32[128,128]{1,0:T(8,128)S(1)}, f32[128,128]{1,0:T(8,128)S(1)}, u32[]{:S(2)}, u32[]{:S(2)}) collective-permute-start(f32[128,128]{1,0:T(8,128)S(1)} %pad_maximum_fusion), channel_id=1, source_target_pairs={{16,0},{24,8},{0,16},{8,24},{17,1},{25,9},{1,17},{9,25},{18,2},{26... | collective-permute-start | bytes 196616 | tf_op jit(solution)/shard_map/ppermute | solution.py:847
  17.2 0.5 %collective-permute-start.5 = (f32[128,128]{1,0:T(8,128)S(1)}, f32[128,128]{1,0:T(8,128)S(1)}, u32[]{:S(2)}, u32[]{:S(2)}) collective-permute-start(f32[128,128]{1,0:T(8,128)S(1)} %pad_maximum_fusion), channel_id=1, source_target_pairs={{24,0},{16,8},{8,16},{0,24},{25,1},{17,9},{9,17},{1,25},{26,2},{18... | collective-permute-start | bytes 196616 | tf_op jit(solution)/shard_map/ppermute | solution.py:847
  17.7 0.0 collective-permute-start.10
  17.7 0.8 %collective-permute-done.3 = f32[128,128]{1,0:T(8,128)S(1)} collective-permute-done((f32[128,128]{1,0:T(8,128)S(1)}, f32[128,128]{1,0:T(8,128)S(1)}, u32[]{:S(2)}, u32[]{:S(2)}) %collective-permute-start.3) | collective-permute-done | bytes 65568 | tf_op jit(solution)/shard_map/ppermute | solution.py:847
  18.5 0.0 collective-permute-start.8
  18.5 1.7 %collective-permute-done.4 = f32[128,128]{1,0:T(8,128)S(1)} collective-permute-done((f32[128,128]{1,0:T(8,128)S(1)}, f32[128,128]{1,0:T(8,128)S(1)}, u32[]{:S(2)}, u32[]{:S(2)}) %collective-permute-start.4) | collective-permute-done | bytes 65568 | tf_op jit(solution)/shard_map/ppermute | solution.py:847
  20.2 0.0 collective-permute-start.9
  20.2 2.2 %collective-permute-done.5 = f32[128,128]{1,0:T(8,128)S(1)} collective-permute-done((f32[128,128]{1,0:T(8,128)S(1)}, f32[128,128]{1,0:T(8,128)S(1)}, u32[]{:S(2)}, u32[]{:S(2)}) %collective-permute-start.5) | collective-permute-done | bytes 65568 | tf_op jit(solution)/shard_map/ppermute | solution.py:847
  22.4 0.0 collective-permute-start.6
  22.4 0.0 collective-permute-done.7.refs_4_
  22.4 0.0 collective-permute-done.10.refs_7_
  22.4 0.0 collective-permute-done.8.refs_5_
  22.4 0.0 collective-permute-done.9.refs_6_
  22.4 2.1 %first.1 = (f32[38,48,128]{2,1,0:T(8,128)S(1)}, f32[1024,128]{1,0:T(8,128)S(1)}, f32[32,128]{1,0:T(8,128)S(1)}, bf16[640,1024]{1,0:T(8,128)(2,1)S(1)}, bf16[1024...) custom-call(f32[168,128]{1,0:T(8,128)S(1)} %pack.1.refs_0_, ...), custom_call_target="tpu_custom_call" | custom-call | flops 3000000000 | tf_op jit(solution)/shard_map/first/pallas_call | solution.py:893
  24.5 1.5 %second.1 = (f32[32,32,128]{2,1,0:T(8,128)S(1)}, f32[32,32,128]{2,1,0:T(8,128)S(1)}, f32[2,128]{1,0:T(2,128)S(1)}) custom-call(f32[38,48,128]{2,1,0:T(8,128)S(1)} %get-tuple-element.13.refs_0_.refs_2_, f32[1024,128]{1,0:T(8,128)S(1)} %get-tuple-element.14.refs_1_, f32[32,128]{1,0:T(8,128)S(1)} %get-tuple-element.15.refs_2_, ...), custom_call_target="tpu_custom_call" | custom-call | flops 2000000000 | tf_op jit(solution)/shard_map/second/pallas_call | solution.py:912
  26.1 0.0 collective-permute-done.6.refs_1_
  26.1 4.5 %step.1 = (f32[1,8,16,128]{3,2,1,0:T(8,128)}, f32[1,8,16,128]{3,2,1,0:T(8,128)}, f32[1]{0:T(128)}) custom-call(f32[512,128]{1,0:T(8,128)S(1)} %constant_dynamic-update-slice_fusion.refs_0_, f32[512,128]{1,0:T(8,128)S(1)} %collective-permute-done.6.refs_1_, f32[38,48,128]{2,1,0:T(8,128)S(1)} %get-tuple-element.13.refs_0_.refs_2_, ...), custom_call_target="tpu_custom_call" | custom-call | flops 6000000000 | tf_op jit(solution)/shard_map/step/pallas_call | solution.py:923
  (8 shorter events, 0.0 us)
Async XLA Ops:
  1.7 12.4 %collective-permute-start.2 = (f32[168,128]{1,0:T(8,128)S(1)}, f32[168,128]{1,0:T(8,128)S(1)}, u32[]{:S(2)}, u32[]{:S(2)}) collective-permute-start(f32[168,128]{1,0:T(8,128)S(1)} %pack.1.refs_0_), channel_id=1, source_target_pairs={{6,0},{4,2},{2,4},{0,6},{7,1},{5,3},{3,5},{1,7},{14,8},{12,10},{10... | collective-permute-start | bytes 258056 | tf_op jit(solution)/shard_map/ppermute | solution.py:847
  6.9 6.2 %collective-permute-start = (f32[168,128]{1,0:T(8,128)S(1)}, f32[168,128]{1,0:T(8,128)S(1)}, u32[]{:S(2)}, u32[]{:S(2)}) collective-permute-start(f32[168,128]{1,0:T(8,128)S(1)} %pack.1.refs_0_), channel_id=1, source_target_pairs={{2,0},{0,2},{6,4},{4,6},{3,1},{1,3},{7,5},{5,7},{10,8},{8,10},{14,... | collective-permute-start | bytes 258056 | tf_op jit(solution)/shard_map/ppermute | solution.py:847
  6.9 7.2 %collective-permute-start.1 = (f32[168,128]{1,0:T(8,128)S(1)}, f32[168,128]{1,0:T(8,128)S(1)}, u32[]{:S(2)}, u32[]{:S(2)}) collective-permute-start(f32[168,128]{1,0:T(8,128)S(1)} %pack.1.refs_0_), channel_id=1, source_target_pairs={{4,0},{6,2},{0,4},{2,6},{5,1},{7,3},{1,5},{3,7},{12,8},{14,10},{8,... | collective-permute-start | bytes 258056 | tf_op jit(solution)/shard_map/ppermute | solution.py:847
  14.1 4.3 %collective-permute-start.3 = (f32[128,128]{1,0:T(8,128)S(1)}, f32[128,128]{1,0:T(8,128)S(1)}, u32[]{:S(2)}, u32[]{:S(2)}) collective-permute-start(f32[128,128]{1,0:T(8,128)S(1)} %pad_maximum_fusion), channel_id=1, source_target_pairs={{8,0},{0,8},{24,16},{16,24},{9,1},{1,9},{25,17},{17,25},{10,2},{2,... | collective-permute-start | bytes 196616 | tf_op jit(solution)/shard_map/ppermute | solution.py:847
  15.7 6.7 %collective-permute-start.7 = (f32[168,128]{1,0:T(8,128)S(1)}, f32[168,128]{1,0:T(8,128)S(1)}, u32[]{:S(2)}, u32[]{:S(2)}) collective-permute-start(f32[168,128]{1,0:T(8,128)S(1)} %pack.1.refs_0_), channel_id=1, source_target_pairs={{1,0},{0,1},{3,2},{2,3},{5,4},{4,5},{7,6},{6,7},{9,8},{8,9},{11,10... | collective-permute-start | bytes 258056 | tf_op jit(solution)/shard_map/ppermute | solution.py:847
  15.7 4.5 %collective-permute-start.4 = (f32[128,128]{1,0:T(8,128)S(1)}, f32[128,128]{1,0:T(8,128)S(1)}, u32[]{:S(2)}, u32[]{:S(2)}) collective-permute-start(f32[128,128]{1,0:T(8,128)S(1)} %pad_maximum_fusion), channel_id=1, source_target_pairs={{16,0},{24,8},{0,16},{8,24},{17,1},{25,9},{1,17},{9,25},{18,2},{26... | collective-permute-start | bytes 196616 | tf_op jit(solution)/shard_map/ppermute | solution.py:847
  17.2 5.2 %collective-permute-start.5 = (f32[128,128]{1,0:T(8,128)S(1)}, f32[128,128]{1,0:T(8,128)S(1)}, u32[]{:S(2)}, u32[]{:S(2)}) collective-permute-start(f32[128,128]{1,0:T(8,128)S(1)} %pad_maximum_fusion), channel_id=1, source_target_pairs={{24,0},{16,8},{8,16},{0,24},{25,1},{17,9},{9,17},{1,25},{26,2},{18... | collective-permute-start | bytes 196616 | tf_op jit(solution)/shard_map/ppermute | solution.py:847
  17.7 4.7 %collective-permute-start.10 = (f32[168,128]{1,0:T(8,128)S(1)}, f32[168,128]{1,0:T(8,128)S(1)}, u32[]{:S(2)}, u32[]{:S(2)}) collective-permute-start(f32[168,128]{1,0:T(8,128)S(1)} %collective-permute-done.2.refs_3_), channel_id=1, source_target_pairs={{1,0},{0,1},{3,2},{2,3},{5,4},{4,5},{7,6},{6,7},{9,8},{8,9},{11,10... | collective-permute-start | bytes 258056 | tf_op jit(solution)/shard_map/ppermute | solution.py:847
  18.5 4.0 %collective-permute-start.8 = (f32[168,128]{1,0:T(8,128)S(1)}, f32[168,128]{1,0:T(8,128)S(1)}, u32[]{:S(2)}, u32[]{:S(2)}) collective-permute-start(f32[168,128]{1,0:T(8,128)S(1)} %collective-permute-done.refs_1_), channel_id=1, source_target_pairs={{1,0},{0,1},{3,2},{2,3},{5,4},{4,5},{7,6},{6,7},{9,8},{8,9},{11,10... | collective-permute-start | bytes 258056 | tf_op jit(solution)/shard_map/ppermute | solution.py:847
  20.2 2.2 %collective-permute-start.9 = (f32[168,128]{1,0:T(8,128)S(1)}, f32[168,128]{1,0:T(8,128)S(1)}, u32[]{:S(2)}, u32[]{:S(2)}) collective-permute-start(f32[168,128]{1,0:T(8,128)S(1)} %collective-permute-done.1.refs_2_), channel_id=1, source_target_pairs={{1,0},{0,1},{3,2},{2,3},{5,4},{4,5},{7,6},{6,7},{9,8},{8,9},{11,10... | collective-permute-start | bytes 258056 | tf_op jit(solution)/shard_map/ppermute | solution.py:847
  22.4 3.7 %collective-permute-start.6 = (f32[512,128]{1,0:T(8,128)S(1)}, f32[512,128]{1,0:T(8,128)S(1)}, u32[]{:S(2)}, u32[]{:S(2)}) collective-permute-start(f32[512,128]{1,0:T(8,128)S(1)} %constant_dynamic-update-slice_fusion.refs_0_), channel_id=1, source_target_pairs={{1,0},{0,1},{3,2},{2,3},{5,4},{4,5},{7,6},{6,7},{9,8},{8,9},{11,10... | collective-permute-start | bytes 786440 | tf_op jit(solution)/shard_map/ppermute | solution.py:847

commit v2 on v1

--- a/solution.py
+++ b/solution.py
@@ -290,7 +290,7 @@
         self.wave_rows = self.tile_x * self.tile_y
         self.pot_rows = self.wave_rows // groups
         self.param_rows = -(-2 * atoms // SUBLANES) * SUBLANES
-        self.rows = self.wave_rows + self.pot_rows + self.param_rows
+        self.rows = self.pot_rows + self.param_rows
         self.factors = len(PLANE_FACTORS) * self.all_atoms
 
     def fits(self, vmem_bytes):
@@ -327,12 +327,12 @@
 META_LANE = 96
 
 
-def pack_kernel(sz, wave_ref, pot_ref, offs_ref, counts_ref, dh_ref, ds_ref, out_ref, *scratch):
+def pack_kernel(sz, pot_ref, offs_ref, counts_ref, dh_ref, ds_ref, wave_ref, out_ref, own_ref, *scratch):
     *places, sems = scratch
     pot, offs, counts, dh, ds = places
-    start, base = sz.wave_rows, sz.wave_rows + sz.pot_rows
+    base = sz.pot_rows
     sources = (pot_ref, offs_ref, counts_ref, dh_ref, ds_ref, wave_ref)
-    places = places + [out_ref.at[pl.ds(0, start)]]
+    places = places + [own_ref]
     copies = [
         pltpu.make_async_copy(a, b, sems.at[i])
         for i, (a, b) in enumerate(zip(sources, places))
@@ -346,7 +346,7 @@
     pieces = [
         pot[g * per : (g + 1) * per].reshape(sz.pot_rows, sz.chunk) for g in range(sz.groups)
     ]
-    out_ref[start:base, :] = pltpu.roll(
+    out_ref[:base, :] = pltpu.roll(
         jnp.concatenate(pieces, axis=1), lax.axis_index("band") * sz.chunk, 1
     )
     for j in range(NPROJ):
@@ -388,10 +388,11 @@
     planes = [at(x, 0) for x in range(-3, count + 3)]
     found = []
     for x in range(count):
-        total = (-1.5 * STENCIL[0]) * planes[x + 3]
+        total = None
         for reach in (1, 2, 3):
             around = (planes[x + 3 - reach] + planes[x + 3 + reach]) + (at(x, -reach) + at(x, reach))
-            total = total + (-0.5 * STENCIL[reach]) * around
+            term = (-0.5 * STENCIL[reach]) * around
+            total = term if total is None else total + term
         found.append((planes[x + 3], total))
     return found
 
@@ -570,26 +571,15 @@
         emit(at, part, halves(dot(a_ref[at : at + part, :], q_ref[...])))
 
 
-def first_kernel(sz, *refs):
-    blocks, refs = refs[: sz.tiles_x * sz.tiles_y], refs[sz.tiles_x * sz.tiles_y :]
-    (psi, zkin, inner_ref, w_ref, a_ref, wz_ref, par_ref, parts, wx_ref, wy_ref) = refs
-    nx, ny = sz.grid_x, sz.grid_y
-    for index, block in enumerate(blocks):
+def weights_kernel(sz, *refs):
+    params, (w_ref, a_ref, wz_ref, par_ref, wx_ref, wy_ref) = refs[: sz.tiles_y], refs[sz.tiles_y :]
+    for index in range(sz.tiles_x * sz.tiles_y):
+        turn_y, turn_x = divmod(index, sz.tiles_x)
         tile_x, tile_y = tile_at(sz, index)
-        at_y = pl.multiple_of(tile_y * sz.tile_y, 16)
-        for x in range(sz.tile_x):
-            value = block[x * sz.tile_y : (x + 1) * sz.tile_y, :]
-            cell_x = tile_x * sz.tile_x + x
-            psi[cell_x + 3, pl.ds(at_y + SUBLANES, sz.tile_y), :] = value
-            rows = pl.ds(pl.multiple_of(cell_x * ny + at_y, 16), sz.tile_y)
-            high, low = split(value)
-            parts[rows, :LANES] = high
-            parts[rows, LANES:] = low
         tile = tile_x * sz.tiles_y + tile_y
         for k in range(2):
-            at = sz.wave_rows + sz.pot_rows + k * sz.atoms
-            par_ref[k, pl.ds(tile * sz.atoms, sz.atoms), :] = block[at : at + sz.atoms, :]
-    fill_rims(psi, 3, nx, ny)
+            at = turn_x * sz.param_rows + k * sz.atoms
+            par_ref[k, pl.ds(tile * sz.atoms, sz.atoms), :] = params[turn_y][at : at + sz.atoms, :]
     owners = lax.broadcasted_iota(jnp.int32, (sz.all_atoms, LANES), 0) // sz.atoms
     lane = lanes_of(sz.all_atoms)
     meta = pltpu.roll(par_ref[0], LANES - META_LANE, 1)
@@ -598,6 +588,25 @@
     par_ref[2] = meta
     depth_weights(meta, wz_ref)
     plane_weights(sz, meta, w_ref, a_ref, wx_ref, wy_ref)
+
+
+def first_kernel(sz, *refs):
+    blocks, refs = refs[: sz.tiles_x * sz.tiles_y], refs[sz.tiles_x * sz.tiles_y :]
+    (w_ref, wz_ref, par_ref, psi, zkin, inner_ref, parts) = refs
+    nx, ny = sz.grid_x, sz.grid_y
+    for index, block in enumerate(blocks):
+        tile_x, tile_y = tile_at(sz, index)
+        at_y = pl.multiple_of(tile_y * sz.tile_y, 16)
+        for x in range(sz.tile_x):
+            value = block[0, x]
+            cell_x = tile_x * sz.tile_x + x
+            psi[cell_x + 3, pl.ds(at_y + SUBLANES, sz.tile_y), :] = value
+            rows = pl.ds(pl.multiple_of(cell_x * ny + at_y, 16), sz.tile_y)
+            high, low = split(value)
+            parts[rows, :LANES] = high
+            parts[rows, LANES:] = low
+    fill_rims(psi, 3, nx, ny)
+    meta = par_ref[2]
     active = active_columns(meta)
     sums = None
     for x0 in range(0, nx, BLOCK):
@@ -625,8 +634,8 @@
     projector_sources(sz, par_ref[0], inner_ref[...], active, wz_ref, q_ref)
     for x0 in range(0, nx, BLOCK):
         for y0 in range(0, ny, SUBLANES):
-            for x, (_, value) in enumerate(planar_kinetic(psi, x0, y0, SUBLANES, BLOCK)):
-                hpsi[x0 + x, y0 : y0 + SUBLANES, :] = value
+            for x, (center, value) in enumerate(planar_kinetic(psi, x0, y0, SUBLANES, BLOCK)):
+                hpsi[x0 + x, y0 : y0 + SUBLANES, :] = value + (-1.5 * STENCIL[0]) * center
     found = []
 
     def emit_h(at, rows, value):
@@ -660,27 +669,36 @@
     return 0.5 / 4.0**level, RELAXATION / diagonal_of(level)
 
 
-def restrict_into(count_x, count_y, level, source, target, rows_ref):
+def restrict_planes(count_x, count_y, level, source, emit):
     spread, guess = level_numbers(level)
-    rows = 2 * SUBLANES
-
-    def body(x0):
-        for y0 in range(0, count_y, rows):
-            found = neighbour_block(source, x0, y0, rows, BLOCK, 2**level)
-            values = [(1.0 - RELAXATION) * c + (spread * guess) * n for c, n in found]
-            for x in range(BLOCK // 2):
-                slot = y0 // rows * (BLOCK // 2) + x
-                rows_ref[slot] = values[2 * x] + values[2 * x + 1]
-                total = (
-                    rows_ref[slot, pl.ds(0, SUBLANES, stride=2), :]
-                    + rows_ref[slot, pl.ds(1, SUBLANES, stride=2), :]
-                )
-                target[x0 // 2 + x + 1, pl.ds(SUBLANES + y0 // 2, SUBLANES), :] = 0.125 * pair_lanes(
-                    total, 2**level
-                )
-
-    over_blocks(count_x, body)
-    fill_rims(target, 1, count_x // 2, count_y // 2)
+    weight, step = spread * guess, 2**level
+    for x in range(count_x // 2):
+        for y0 in range(0, count_y // 2, SUBLANES):
+            at = lambda dx, dy: source[
+                2 * x + dx + 1, pl.ds(SUBLANES + 2 * y0 + dy, SUBLANES, stride=2), :
+            ]
+            inside = (at(0, 0) + at(0, 1)) + (at(1, 0) + at(1, 1))
+            beside = (at(-1, 0) + at(-1, 1)) + (at(2, 0) + at(2, 1))
+            beside = beside + ((at(0, -1) + at(1, -1)) + (at(0, 2) + at(1, 2)))
+            beside = beside + shifted_pair(inside, step)
+            total = (0.125 * (1.0 - RELAXATION + 2.0 * weight)) * inside + (0.125 * weight) * beside
+            emit(x, y0, pair_lanes(total, step))
+
+
+def coarsest(source):
+    spread, guess = level_numbers(2)
+    count, rows = len(source), source[0].shape[0]
+    planes = [guess * b for b in source]
+    for _ in range(COARSE_SWEEPS):
+        fresh = []
+        for x, b in enumerate(source):
+            center = planes[x]
+            around = planes[x - 1] + planes[(x + 1) % count]
+            around = around + (pltpu.roll(center, 1, 0) + pltpu.roll(center, rows - 1, 0))
+            around = around + shifted_pair(center, 4)
+            fresh.append((1.0 - RELAXATION) * center + guess * b + (guess * spread) * around)
+        planes = fresh
+    return planes
 
 
 def relax_rows(count_x, count_y, level, guess_ref, source, emit, after_block=lambda x0: None):
@@ -752,7 +770,7 @@
     pots, refs = refs[: sz.tiles_y], refs[sz.tiles_y :]
     (psi, hpsi, spsi, w_ref, a_ref, wz_ref, par_ref, sums_ref), refs = refs[:8], refs[8:]
     (bands_ref, resid_ref, energy_ref), refs = refs[:3], refs[3:]
-    (pot, res, zfield, direct, change, b1, z1, x1, b2, x2, rows_ref, parts, q_ref, zkin, tile_sums) = refs
+    (pot, res, zfield, direct, change, b1, z1, x1, parts, q_ref, zkin, tile_sums) = refs
     nx, ny = sz.grid_x, sz.grid_y
     here_x, here_y = lax.axis_index("dx"), lax.axis_index("dy")
     total = place_potential(sz, pots, psi, pot, tile_sums)
@@ -763,21 +781,28 @@
         for x in range(BLOCK):
             center = psi[x0 + x + 3, pl.ds(SUBLANES, ny), :]
             value = hpsi[x0 + x] + pot[x0 + x] * center - energy * spsi[x0 + x]
+            pot[x0 + x] = pot[x0 + x] + (-1.5 * STENCIL[0] - energy)
             res[x0 + x + 1, pl.ds(SUBLANES, ny), :] = value
 
     over_blocks(nx, residual)
     fill_rims(res, 1, nx, ny)
-    restrict_into(nx, ny, 0, res, b1, rows_ref)
-    restrict_into(nx // 2, ny // 2, 1, b1, b2, rows_ref)
-    quarter_x, quarter_y = nx // 4, ny // 4
-    x2[...] = level_numbers(2)[1] * b2[...]
-    for _ in range(COARSE_SWEEPS):
-        planes = []
-        relax_rows(quarter_x, quarter_y, 2, x2, b2, lambda *piece: planes.append(piece))
-        for x, y0, rows, value in planes:
-            x2[x + 1, pl.ds(SUBLANES + y0, rows), :] = value
-        fill_rims(x2, 1, quarter_x, quarter_y)
-    coarse_two = lambda x, y: x2[x + 1, pl.ds(SUBLANES + y, SUBLANES), :]
+
+    def emit_b1(x, y0, value):
+        b1[x + 1, SUBLANES + y0 : 2 * SUBLANES + y0, :] = value
+
+    restrict_planes(nx, ny, 0, res, emit_b1)
+    fill_rims(b1, 1, nx // 2, ny // 2)
+    pieces = {}
+
+    def emit_b2(x, y0, value):
+        pieces[x, y0] = value
+
+    restrict_planes(nx // 2, ny // 2, 1, b1, emit_b2)
+    tops = range(0, ny // 4, SUBLANES)
+    planes = coarsest(
+        [jnp.concatenate([pieces[x, y0] for y0 in tops], axis=0) for x in range(nx // 4)]
+    )
+    coarse_two = lambda x, y: planes[x][y : y + SUBLANES]
     prolong_into(nx // 2, ny // 2, 1, coarse_two, b1, z1)
 
     def emit_one(x, y0, rows, value):
@@ -809,7 +834,7 @@
         for y0 in range(0, ny, SUBLANES):
             for x, (center, value) in enumerate(planar_kinetic(direct, x0, y0, SUBLANES, BLOCK)):
                 rows = slice(y0, y0 + SUBLANES)
-                change[x0 + x, rows, :] = value + (pot[x0 + x, rows, :] - energy) * center
+                change[x0 + x, rows, :] = value + pot[x0 + x, rows, :] * center
     q_ref[sz.factors :, LANES:] = jnp.zeros((sz.factors, LANES), jnp.bfloat16)
     matrix = par_ref[0] - energy * par_ref[1]
     projector_sources(sz, matrix, inner_lanes(columns), active, wz_ref, q_ref)
@@ -858,57 +883,65 @@
     grant = pltpu.CompilerParams(vmem_limit_bytes=VMEM_GRANT)
     cost = lambda flops: pl.CostEstimate(flops=flops, transcendentals=0, bytes_accessed=0)
     inputs = (
-        wave_bands.reshape(sz.wave_rows, LANES),
         potential,
         atom_offsets.transpose(0, 3, 1, 2),
         proj_counts,
         dh_matrix.transpose(0, 1, 3, 2, 4),
         ds_matrix.transpose(0, 1, 3, 2, 4),
-    )
-    own = pl.pallas_call(
+        wave_bands,
+    )
+    own, wave = pl.pallas_call(
         functools.partial(pack_kernel, sz),
-        out_shape=shape(sz.rows, LANES),
+        out_shape=(shape(sz.rows, LANES), shape(*wave_bands.shape)),
         in_specs=[hbm] * 6,
-        out_specs=vmem,
+        out_specs=(vmem, vmem),
         scratch_shapes=[
-            scratch(*inputs[1].shape),
+            scratch(*inputs[0].shape),
+            pltpu.SMEM(inputs[1].shape, jnp.int32),
             pltpu.SMEM(inputs[2].shape, jnp.int32),
-            pltpu.SMEM(inputs[3].shape, jnp.int32),
+            scratch(*inputs[3].shape),
             scratch(*inputs[4].shape),
-            scratch(*inputs[5].shape),
             pltpu.SemaphoreType.DMA((6,)),
         ],
         compiler_params=grant,
         name="pack",
     )(*(pltpu.with_memory_space_constraint(value, pltpu.HBM) for value in inputs))
-    line = gathered(own, "dx")
+    small = gathered(own, "dx")
+    line = gathered(wave, "dx")
+    chunk = jnp.concatenate([block[: sz.pot_rows] for block in small], axis=0)
+    chunks = jnp.concatenate(gathered(chunk, "band"), axis=0)
+    params = gathered(jnp.concatenate([block[sz.pot_rows :] for block in small], axis=0), "dy")
     crossed = [gathered(block, "dy") for block in line]
     blocks = [each[turn] for turn in range(sz.tiles_y) for each in crossed]
-    pieces = [block[sz.wave_rows : sz.wave_rows + sz.pot_rows] for block in line]
-    chunks = jnp.concatenate(gathered(jnp.concatenate(pieces, axis=0), "band"), axis=0)
     pots = gathered(chunks, "dy")
     nx, ny = sz.grid_x, sz.grid_y
     padded = lambda x, y, width: (x + 2 * width, y + 2 * SUBLANES, LANES)
     q_scratch = pltpu.VMEM((2 * sz.factors, 2 * LANES), jnp.bfloat16)
-    psi, zkin, inner, w, a, wz, par = pl.pallas_call(
-        functools.partial(first_kernel, sz),
+    w, a, wz, par = pl.pallas_call(
+        functools.partial(weights_kernel, sz),
         out_shape=(
-            shape(*padded(nx, ny, 3)),
-            shape(sz.cells, LANES),
-            shape(sz.all_atoms, LANES),
             half(2 * sz.factors, sz.cells),
             half(sz.cells, 2 * sz.factors),
             shape(6, sz.all_atoms, LANES),
             shape(3, sz.all_atoms, LANES),
         ),
-        in_specs=[vmem] * len(blocks),
-        out_specs=(vmem,) * 7,
-        scratch_shapes=[pltpu.VMEM((sz.cells, 2 * LANES), jnp.bfloat16)]
-        + [scratch(2 * sz.factors // LANES, n, LANES) for n in (nx, ny)],
+        in_specs=[vmem] * len(params),
+        out_specs=(vmem,) * 4,
+        scratch_shapes=[scratch(2 * sz.factors // LANES, n, LANES) for n in (nx, ny)],
         compiler_params=grant,
-        cost_estimate=cost(3_000_000_000),
+        cost_estimate=cost(1_000_000_000),
+        name="weights",
+    )(*params)
+    psi, zkin, inner = pl.pallas_call(
+        functools.partial(first_kernel, sz),
+        out_shape=(shape(*padded(nx, ny, 3)), shape(sz.cells, LANES), shape(sz.all_atoms, LANES)),
+        in_specs=[vmem] * (len(blocks) + 3),
+        out_specs=(vmem,) * 3,
+        scratch_shapes=[pltpu.VMEM((sz.cells, 2 * LANES), jnp.bfloat16)],
+        compiler_params=grant,
+        cost_estimate=cost(2_000_000_000),
         name="first",
-    )(*blocks)
+    )(*blocks, w, wz, par)
     hpsi, spsi, sums = pl.pallas_call(
         functools.partial(second_kernel, sz),
         out_shape=(shape(nx, ny, LANES), shape(nx, ny, LANES), shape(2, LANES)),
@@ -938,9 +971,6 @@
             scratch(*padded(nx // 2, ny // 2, 1)),
             scratch(*padded(nx // 2, ny // 2, 1)),
             scratch(nx // 2, ny // 2, LANES),
-            scratch(*padded(nx // 4, ny // 4, 1)),
-            scratch(*padded(nx // 4, ny // 4, 1)),
-            scratch(ny // 2 // SUBLANES * (BLOCK // 2), 2 * SUBLANES, LANES),
             pltpu.VMEM((sz.cells, 2 * LANES), jnp.bfloat16),
             pltpu.VMEM((2 * sz.factors, 2 * LANES), jnp.bfloat16),
             scratch(sz.cells, LANES),

time: 30.7 us -> 32.4 us (1.055)
  starting transfers between devices: 9.35 us -> 15.3 us
  waiting for transfers between devices: 11.2 us -> 7.01 us
    ppermute x11 -> x15, starting transfers between devices: 9.35 us -> 15.3 us  [gathered(): found.append(lax.ppermute(value, axis, pairs(turn)))]
    ppermute x11 -> x15, waiting for transfers between devices: 11.2 us -> 7.01 us  [gathered(): found.append(lax.ppermute(value, axis, pairs(turn)))]
    pallas_call x1 -> x2, Pallas kernels: 1.11 us -> 2.23 us  [the longest x1 1.13 us: replicated(): pl.pallas_call(functools.partial(weights_kernel, sz), out_shape=(half(2 *...]
    pallas_call x1, Pallas kernels: 2.08 us -> 1.01 us  [replicated(): pl.pallas_call(functools.partial(first_kernel, sz), out_shape=(shape(*pad...]
  transfers between devices with their start and end apart: 11 -> 15, of which waited for: 5 -> 5; matrix products, arithmetic and copies ran while one was open for 0% -> 0% of each run, Pallas kernels for 12% -> 11%
where the time goes in v2:
time: 32.4 us; the launch traced here: 32.2 us
  starting transfers between devices  15.3 us (47%)
  Pallas kernels  9.08 us (28%)
  waiting for transfers between devices  7.01 us (22%)
  between operations  0.8 us (2%)
    ppermute x15, starting transfers between devices, gathered(): found.append(lax.ppermute(value, axis, pairs(turn)))  15.3 us
    ppermute x15, waiting for transfers between devices, gathered(): found.append(lax.ppermute(value, axis, pairs(turn)))  7.01 us
    pallas_call x1, Pallas kernels, replicated(): pl.pallas_call(functools.partial(step_kernel, sz), out_shape=(jax.ShapeDt...  4.3 us
    pallas_call x1, Pallas kernels, replicated(): pl.pallas_call(functools.partial(second_kernel, sz), out_shape=(shape(nx,...  1.53 us
    pallas_call x1, Pallas kernels, replicated(): pl.pallas_call(functools.partial(weights_kernel, sz), out_shape=(half(2 *...  1.13 us
    pallas_call x1, Pallas kernels, replicated(): pl.pallas_call(functools.partial(pack_kernel, sz), out_shape=(shape(sz.ro...  1.11 us
    pallas_call x1, Pallas kernels, replicated(): pl.pallas_call(functools.partial(first_kernel, sz), out_shape=(shape(*pad...  1.01 us
  transfers between devices with their start and end apart: 15, of which 5 were waited for; matrix products, arithmetic and copies ran while one was open for 0% of the time, Pallas kernels for 11%

profile of v2, /device:TPU:0, one launch (start us, length us, event | category | flops | bytes accessed | tf_op | source)
XLA Modules:
  0.0 32.2 jit_solution(11327478697312865291)
XLA Ops:
  0.6 1.1 %pack.1 = (f32[40,128]{1,0:T(8,128)S(1)}, f32[1,8,16,128]{3,2,1,0:T(8,128)S(1)}) custom-call(f32[8,16,32]{2,1,0:T(8,128)} %pot_ref.1, s32[1,3,1,4]{3,2,1,0:T(1,128)} %bitcast.5, s32[1,1,4]{2,1,0:T(1,128)} %counts_ref.1, f32[1,1,9,4,9]{4,3,2,1,0:T(4,128)} %bitcast.3, f32[1,1,9,4,9]{4,3,2,1,0:T(4,128)} %bitcast.4, f32[1,8,16,128]{3,2,1,0:T(8,128)} %wave_ref.1), custom_call_target="tpu_custom_call" | custom-call | tf_op jit(solution)/shard_map/pack/pallas_call | solution.py:893
  1.7 3.1 %collective-permute-start = (f32[40,128]{1,0:T(8,128)S(1)}, f32[40,128]{1,0:T(8,128)S(1)}, u32[]{:S(2)}, u32[]{:S(2)}) collective-permute-start(f32[40,128]{1,0:T(8,128)S(1)} %get-tuple-element.15), channel_id=1, source_target_pairs={{2,0},{0,2},{6,4},{4,6},{3,1},{1,3},{7,5},{5,7},{10,8},{8,10},{14,... | collective-permute-start | bytes 61448 | tf_op jit(solution)/shard_map/ppermute | solution.py:872
  4.9 2.6 %collective-permute-start.1 = (f32[40,128]{1,0:T(8,128)S(1)}, f32[40,128]{1,0:T(8,128)S(1)}, u32[]{:S(2)}, u32[]{:S(2)}) collective-permute-start(f32[40,128]{1,0:T(8,128)S(1)} %get-tuple-element.15), channel_id=1, source_target_pairs={{4,0},{6,2},{0,4},{2,6},{5,1},{7,3},{1,5},{3,7},{12,8},{14,10},{8,... | collective-permute-start | bytes 61448 | tf_op jit(solution)/shard_map/ppermute | solution.py:872
  7.5 0.0 collective-permute-start.2
  7.5 0.9 %collective-permute-start.7 = (f32[1,8,16,128]{3,2,1,0:T(8,128)S(1)}, f32[1,8,16,128]{3,2,1,0:T(8,128)S(1)}, u32[]{:S(2)}, u32[]{:S(2)}) collective-permute-start(f32[1,8,16,128]{3,2,1,0:T(8,128)S(1)} %get-tuple-element.16.refs_0_), channel_id=1, source_target_pairs={{2,0},{0,2},{6,4},{4,6},{3,1},{1,3},{7,5},{5,7},{10,8},{8,10},{14,... | collective-permute-start | bytes 196616 | tf_op jit(solution)/shard_map/ppermute | solution.py:872
  8.4 3.5 %collective-permute-start.8 = (f32[1,8,16,128]{3,2,1,0:T(8,128)S(1)}, f32[1,8,16,128]{3,2,1,0:T(8,128)S(1)}, u32[]{:S(2)}, u32[]{:S(2)}) collective-permute-start(f32[1,8,16,128]{3,2,1,0:T(8,128)S(1)} %get-tuple-element.16.refs_0_), channel_id=1, source_target_pairs={{4,0},{6,2},{0,4},{2,6},{5,1},{7,3},{1,5},{3,7},{12,8},{14,10},{8,... | collective-permute-start | bytes 196616 | tf_op jit(solution)/shard_map/ppermute | solution.py:872
  11.8 0.0 collective-permute-done
  11.9 0.1 collective-permute-start.9
  11.9 0.0 collective-permute-done.1
  12.0 0.1 collective-permute-start.10
  12.0 1.0 %collective-permute-done.2 = f32[40,128]{1,0:T(8,128)S(1)} collective-permute-done((f32[40,128]{1,0:T(8,128)S(1)}, f32[40,128]{1,0:T(8,128)S(1)}, u32[]{:S(2)}, u32[]{:S(2)}) %collective-permute-start.2) | collective-permute-done | bytes 20512 | tf_op jit(solution)/shard_map/ppermute | solution.py:872
  13.1 0.0 collective-permute-start.14
  13.1 1.1 %collective-permute-done.14.refs_1_ = f32[32,128]{1,0:T(8,128)S(1)} collective-permute-done((f32[32,128]{1,0:T(8,128)S(1)}, f32[32,128]{1,0:T(8,128)S(1)}, u32[]{:S(2)}, u32[]{:S(2)}) %collective-permute-start.14) | collective-permute-done | bytes 16416 | tf_op jit(solution)/shard_map/ppermute | solution.py:872
  14.3 1.5 %collective-permute-start.3 = (f32[128,128]{1,0:T(8,128)S(1)}, f32[128,128]{1,0:T(8,128)S(1)}, u32[]{:S(2)}, u32[]{:S(2)}) collective-permute-start(f32[128,128]{1,0:T(8,128)S(1)} %pad_maximum_fusion), channel_id=1, source_target_pairs={{8,0},{0,8},{24,16},{16,24},{9,1},{1,9},{25,17},{17,25},{10,2},{2,... | collective-permute-start | bytes 196616 | tf_op jit(solution)/shard_map/ppermute | solution.py:872
  15.8 1.1 %weights.1 = (bf16[640,1024]{1,0:T(8,128)(2,1)S(1)}, bf16[1024,640]{1,0:T(8,128)(2,1)S(1)}, f32[6,32,128]{2,1,0:T(8,128)S(1)}, f32[3,32,128]{2,1,0:T(8,128)S(1)}) custom-call(f32[32,128]{1,0:T(8,128)S(1)} %pad_maximum_fusion.1.refs_0_, f32[32,128]{1,0:T(8,128)S(1)} %collective-permute-done.14.refs_1_), custom_call_target="tpu_custom_call" | custom-call | flops 1000000000 | tf_op jit(solution)/shard_map/weights/pallas_call | solution.py:920
  16.9 1.6 %collective-permute-done.3 = f32[128,128]{1,0:T(8,128)S(1)} collective-permute-done((f32[128,128]{1,0:T(8,128)S(1)}, f32[128,128]{1,0:T(8,128)S(1)}, u32[]{:S(2)}, u32[]{:S(2)}) %collective-permute-start.3) | collective-permute-done | bytes 65568 | tf_op jit(solution)/shard_map/ppermute | solution.py:872
  18.5 1.5 %collective-permute-start.4 = (f32[128,128]{1,0:T(8,128)S(1)}, f32[128,128]{1,0:T(8,128)S(1)}, u32[]{:S(2)}, u32[]{:S(2)}) collective-permute-start(f32[128,128]{1,0:T(8,128)S(1)} %pad_maximum_fusion), channel_id=1, source_target_pairs={{16,0},{24,8},{0,16},{8,24},{17,1},{25,9},{1,17},{9,25},{18,2},{26... | collective-permute-start | bytes 196616 | tf_op jit(solution)/shard_map/ppermute | solution.py:872
  20.1 0.0 collective-permute-done.7.refs_1_
  20.1 1.5 %collective-permute-start.5 = (f32[128,128]{1,0:T(8,128)S(1)}, f32[128,128]{1,0:T(8,128)S(1)}, u32[]{:S(2)}, u32[]{:S(2)}) collective-permute-start(f32[128,128]{1,0:T(8,128)S(1)} %pad_maximum_fusion), channel_id=1, source_target_pairs={{24,0},{16,8},{8,16},{0,24},{25,1},{17,9},{9,17},{1,25},{26,2},{18... | collective-permute-start | bytes 196616 | tf_op jit(solution)/shard_map/ppermute | solution.py:872
  21.6 0.0 collective-permute-done.8.refs_2_
  21.6 0.0 collective-permute-start.11
  21.6 0.0 collective-permute-done.9.refs_3_
  21.6 0.5 %collective-permute-start.12 = (f32[1,8,16,128]{3,2,1,0:T(8,128)S(1)}, f32[1,8,16,128]{3,2,1,0:T(8,128)S(1)}, u32[]{:S(2)}, u32[]{:S(2)}) collective-permute-start(f32[1,8,16,128]{3,2,1,0:T(8,128)S(1)} %collective-permute-done.8.refs_2_), channel_id=1, source_target_pairs={{1,0},{0,1},{3,2},{2,3},{5,4},{4,5},{7,6},{6,7},{9,8},{8,9},{11,10... | collective-permute-start | bytes 196616 | tf_op jit(solution)/shard_map/ppermute | solution.py:872
  22.1 1.4 %collective-permute-done.4 = f32[128,128]{1,0:T(8,128)S(1)} collective-permute-done((f32[128,128]{1,0:T(8,128)S(1)}, f32[128,128]{1,0:T(8,128)S(1)}, u32[]{:S(2)}, u32[]{:S(2)}) %collective-permute-start.4) | collective-permute-done | bytes 65568 | tf_op jit(solution)/shard_map/ppermute | solution.py:872
  23.5 0.0 collective-permute-start.13
  23.5 1.8 %collective-permute-done.5 = f32[128,128]{1,0:T(8,128)S(1)} collective-permute-done((f32[128,128]{1,0:T(8,128)S(1)}, f32[128,128]{1,0:T(8,128)S(1)}, u32[]{:S(2)}, u32[]{:S(2)}) %collective-permute-start.5) | collective-permute-done | bytes 65568 | tf_op jit(solution)/shard_map/ppermute | solution.py:872
  25.3 0.0 collective-permute-start.6
  25.3 0.0 collective-permute-done.10.refs_4_
  25.3 0.0 collective-permute-done.11.refs_5_
  25.3 0.0 collective-permute-done.12.refs_6_
  25.3 0.0 collective-permute-done.13.refs_7_
  25.3 1.0 %first.1 = (f32[38,48,128]{2,1,0:T(8,128)S(1)}, f32[1024,128]{1,0:T(8,128)S(1)}, f32[32,128]{1,0:T(8,128)S(1)}) custom-call(f32[1,8,16,128]{3,2,1,0:T(8,128)S(1)} %get-tuple-element.16.refs_0_, f32[1,8,16,128]{3,2,1,0:T(8,128)S(1)} %collective-permute-done.7.refs_1_, f32[1,8,16,128]{3,2,1,0:T(8,128)S(1)} %collective-permute-done.8.refs_2_, ...), custom_call_target="tpu_custom_call" | custom-call | flops 2000000000 | tf_op jit(solution)/shard_map/first/pallas_call | solution.py:935
  26.4 1.5 %second.1 = (f32[32,32,128]{2,1,0:T(8,128)S(1)}, f32[32,32,128]{2,1,0:T(8,128)S(1)}, f32[2,128]{1,0:T(2,128)S(1)}) custom-call(f32[38,48,128]{2,1,0:T(8,128)S(1)} %get-tuple-element.20.refs_0_.refs_2_, f32[1024,128]{1,0:T(8,128)S(1)} %get-tuple-element.21.refs_1_, f32[32,128]{1,0:T(8,128)S(1)} %get-tuple-element.22.refs_2_, ...), custom_call_target="tpu_custom_call" | custom-call | flops 2000000000 | tf_op jit(solution)/shard_map/second/pallas_call | solution.py:945
  27.9 0.0 collective-permute-done.6.refs_1_
  27.9 4.3 %step.1 = (f32[1,8,16,128]{3,2,1,0:T(8,128)}, f32[1,8,16,128]{3,2,1,0:T(8,128)}, f32[1]{0:T(128)}) custom-call(f32[512,128]{1,0:T(8,128)S(1)} %constant_dynamic-update-slice_fusion.refs_0_, f32[512,128]{1,0:T(8,128)S(1)} %collective-permute-done.6.refs_1_, f32[38,48,128]{2,1,0:T(8,128)S(1)} %get-tuple-element.20.refs_0_.refs_2_, ...), custom_call_target="tpu_custom_call" | custom-call | flops 6000000000 | tf_op jit(solution)/shard_map/step/pallas_call | solution.py:956
  (13 shorter events, 0.1 us)
Async XLA Ops:
  1.7 10.1 %collective-permute-start = (f32[40,128]{1,0:T(8,128)S(1)}, f32[40,128]{1,0:T(8,128)S(1)}, u32[]{:S(2)}, u32[]{:S(2)}) collective-permute-start(f32[40,128]{1,0:T(8,128)S(1)} %get-tuple-element.15), channel_id=1, source_target_pairs={{2,0},{0,2},{6,4},{4,6},{3,1},{1,3},{7,5},{5,7},{10,8},{8,10},{14,... | collective-permute-start | bytes 61448 | tf_op jit(solution)/shard_map/ppermute | solution.py:872
  4.9 7.1 %collective-permute-start.1 = (f32[40,128]{1,0:T(8,128)S(1)}, f32[40,128]{1,0:T(8,128)S(1)}, u32[]{:S(2)}, u32[]{:S(2)}) collective-permute-start(f32[40,128]{1,0:T(8,128)S(1)} %get-tuple-element.15), channel_id=1, source_target_pairs={{4,0},{6,2},{0,4},{2,6},{5,1},{7,3},{1,5},{3,7},{12,8},{14,10},{8,... | collective-permute-start | bytes 61448 | tf_op jit(solution)/shard_map/ppermute | solution.py:872
  7.5 5.6 %collective-permute-start.2 = (f32[40,128]{1,0:T(8,128)S(1)}, f32[40,128]{1,0:T(8,128)S(1)}, u32[]{:S(2)}, u32[]{:S(2)}) collective-permute-start(f32[40,128]{1,0:T(8,128)S(1)} %get-tuple-element.15), channel_id=1, source_target_pairs={{6,0},{4,2},{2,4},{0,6},{7,1},{5,3},{3,5},{1,7},{14,8},{12,10},{10... | collective-permute-start | bytes 61448 | tf_op jit(solution)/shard_map/ppermute | solution.py:872
  7.5 12.6 %collective-permute-start.7 = (f32[1,8,16,128]{3,2,1,0:T(8,128)S(1)}, f32[1,8,16,128]{3,2,1,0:T(8,128)S(1)}, u32[]{:S(2)}, u32[]{:S(2)}) collective-permute-start(f32[1,8,16,128]{3,2,1,0:T(8,128)S(1)} %get-tuple-element.16.refs_0_), channel_id=1, source_target_pairs={{2,0},{0,2},{6,4},{4,6},{3,1},{1,3},{7,5},{5,7},{10,8},{8,10},{14,... | collective-permute-start | bytes 196616 | tf_op jit(solution)/shard_map/ppermute | solution.py:872
  8.4 13.2 %collective-permute-start.8 = (f32[1,8,16,128]{3,2,1,0:T(8,128)S(1)}, f32[1,8,16,128]{3,2,1,0:T(8,128)S(1)}, u32[]{:S(2)}, u32[]{:S(2)}) collective-permute-start(f32[1,8,16,128]{3,2,1,0:T(8,128)S(1)} %get-tuple-element.16.refs_0_), channel_id=1, source_target_pairs={{4,0},{6,2},{0,4},{2,6},{5,1},{7,3},{1,5},{3,7},{12,8},{14,10},{8,... | collective-permute-start | bytes 196616 | tf_op jit(solution)/shard_map/ppermute | solution.py:872
  11.9 9.7 %collective-permute-start.9 = (f32[1,8,16,128]{3,2,1,0:T(8,128)S(1)}, f32[1,8,16,128]{3,2,1,0:T(8,128)S(1)}, u32[]{:S(2)}, u32[]{:S(2)}) collective-permute-start(f32[1,8,16,128]{3,2,1,0:T(8,128)S(1)} %get-tuple-element.16.refs_0_), channel_id=1, source_target_pairs={{6,0},{4,2},{2,4},{0,6},{7,1},{5,3},{3,5},{1,7},{14,8},{12,10},{10... | collective-permute-start | bytes 196616 | tf_op jit(solution)/shard_map/ppermute | solution.py:872
  12.0 13.3 %collective-permute-start.10 = (f32[1,8,16,128]{3,2,1,0:T(8,128)S(1)}, f32[1,8,16,128]{3,2,1,0:T(8,128)S(1)}, u32[]{:S(2)}, u32[]{:S(2)}) collective-permute-start(f32[1,8,16,128]{3,2,1,0:T(8,128)S(1)} %get-tuple-element.16.refs_0_), channel_id=1, source_target_pairs={{1,0},{0,1},{3,2},{2,3},{5,4},{4,5},{7,6},{6,7},{9,8},{8,9},{11,10... | collective-permute-start | bytes 196616 | tf_op jit(solution)/shard_map/ppermute | solution.py:872
  13.1 1.2 %collective-permute-start.14 = (f32[32,128]{1,0:T(8,128)S(1)}, f32[32,128]{1,0:T(8,128)S(1)}, u32[]{:S(2)}, u32[]{:S(2)}) collective-permute-start(f32[32,128]{1,0:T(8,128)S(1)} %pad_maximum_fusion.1.refs_0_), channel_id=1, source_target_pairs={{1,0},{0,1},{3,2},{2,3},{5,4},{4,5},{7,6},{6,7},{9,8},{8,9},{11,10... | collective-permute-start | bytes 49160 | tf_op jit(solution)/shard_map/ppermute | solution.py:872
  14.3 4.3 %collective-permute-start.3 = (f32[128,128]{1,0:T(8,128)S(1)}, f32[128,128]{1,0:T(8,128)S(1)}, u32[]{:S(2)}, u32[]{:S(2)}) collective-permute-start(f32[128,128]{1,0:T(8,128)S(1)} %pad_maximum_fusion), channel_id=1, source_target_pairs={{8,0},{0,8},{24,16},{16,24},{9,1},{1,9},{25,17},{17,25},{10,2},{2,... | collective-permute-start | bytes 196616 | tf_op jit(solution)/shard_map/ppermute | solution.py:872
  18.5 5.0 %collective-permute-start.4 = (f32[128,128]{1,0:T(8,128)S(1)}, f32[128,128]{1,0:T(8,128)S(1)}, u32[]{:S(2)}, u32[]{:S(2)}) collective-permute-start(f32[128,128]{1,0:T(8,128)S(1)} %pad_maximum_fusion), channel_id=1, source_target_pairs={{16,0},{24,8},{0,16},{8,24},{17,1},{25,9},{1,17},{9,25},{18,2},{26... | collective-permute-start | bytes 196616 | tf_op jit(solution)/shard_map/ppermute | solution.py:872
  20.1 5.2 %collective-permute-start.5 = (f32[128,128]{1,0:T(8,128)S(1)}, f32[128,128]{1,0:T(8,128)S(1)}, u32[]{:S(2)}, u32[]{:S(2)}) collective-permute-start(f32[128,128]{1,0:T(8,128)S(1)} %pad_maximum_fusion), channel_id=1, source_target_pairs={{24,0},{16,8},{8,16},{0,24},{25,1},{17,9},{9,17},{1,25},{26,2},{18... | collective-permute-start | bytes 196616 | tf_op jit(solution)/shard_map/ppermute | solution.py:872
  21.6 3.8 %collective-permute-start.11 = (f32[1,8,16,128]{3,2,1,0:T(8,128)S(1)}, f32[1,8,16,128]{3,2,1,0:T(8,128)S(1)}, u32[]{:S(2)}, u32[]{:S(2)}) collective-permute-start(f32[1,8,16,128]{3,2,1,0:T(8,128)S(1)} %collective-permute-done.7.refs_1_), channel_id=1, source_target_pairs={{1,0},{0,1},{3,2},{2,3},{5,4},{4,5},{7,6},{6,7},{9,8},{8,9},{11,10... | collective-permute-start | bytes 196616 | tf_op jit(solution)/shard_map/ppermute | solution.py:872
  21.6 3.8 %collective-permute-start.12 = (f32[1,8,16,128]{3,2,1,0:T(8,128)S(1)}, f32[1,8,16,128]{3,2,1,0:T(8,128)S(1)}, u32[]{:S(2)}, u32[]{:S(2)}) collective-permute-start(f32[1,8,16,128]{3,2,1,0:T(8,128)S(1)} %collective-permute-done.8.refs_2_), channel_id=1, source_target_pairs={{1,0},{0,1},{3,2},{2,3},{5,4},{4,5},{7,6},{6,7},{9,8},{8,9},{11,10... | collective-permute-start | bytes 196616 | tf_op jit(solution)/shard_map/ppermute | solution.py:872
  23.5 1.8 %collective-permute-start.13 = (f32[1,8,16,128]{3,2,1,0:T(8,128)S(1)}, f32[1,8,16,128]{3,2,1,0:T(8,128)S(1)}, u32[]{:S(2)}, u32[]{:S(2)}) collective-permute-start(f32[1,8,16,128]{3,2,1,0:T(8,128)S(1)} %collective-permute-done.9.refs_3_), channel_id=1, source_target_pairs={{1,0},{0,1},{3,2},{2,3},{5,4},{4,5},{7,6},{6,7},{9,8},{8,9},{11,10... | collective-permute-start | bytes 196616 | tf_op jit(solution)/shard_map/ppermute | solution.py:872
  25.3 2.6 %collective-permute-start.6 = (f32[512,128]{1,0:T(8,128)S(1)}, f32[512,128]{1,0:T(8,128)S(1)}, u32[]{:S(2)}, u32[]{:S(2)}) collective-permute-start(f32[512,128]{1,0:T(8,128)S(1)} %constant_dynamic-update-slice_fusion.refs_0_), channel_id=1, source_target_pairs={{1,0},{0,1},{3,2},{2,3},{5,4},{4,5},{7,6},{6,7},{9,8},{8,9},{11,10... | collective-permute-start | bytes 786440 | tf_op jit(solution)/shard_map/ppermute | solution.py:872

commit v3 on v2

--- a/solution.py
+++ b/solution.py
@@ -274,6 +274,7 @@
 D_SCALE = 0.28867513
 DEPTH_SCALE = 180.0
 BLOCK = 8
+LUMP = 2
 VMEM_BUDGET = 40 * 1024 * 1024
 VMEM_GRANT = 24 * 1024 * 1024
 
@@ -494,8 +495,8 @@
     wz_ref[5] = radial[2] * (offset * offset)
 
 
-def plane_sums(sz, w_ref, parts, x0):
-    cells = slice(x0 * sz.grid_y, (x0 + BLOCK) * sz.grid_y)
+def plane_sums(sz, w_ref, parts, x0, x1):
+    cells = slice(x0 * sz.grid_y, x1 * sz.grid_y)
     field = parts[cells, :]
     sums = dot(w_ref[:, cells], field)
     return halves(sums[: sz.factors]) + sums[sz.factors :, :LANES]
@@ -610,7 +611,7 @@
     active = active_columns(meta)
     sums = None
     for x0 in range(0, nx, BLOCK):
-        term = plane_sums(sz, w_ref, parts, x0)
+        term = plane_sums(sz, w_ref, parts, x0, x0 + BLOCK)
         sums = term if sums is None else sums + term
     columns = intersections(sz, sums, wz_ref, active)
     zkin[...] = dot(parts[...], depth_matrix())
@@ -818,13 +819,16 @@
         parts[cells, :LANES] = high
         parts[cells, LANES:] = low
 
-    found = []
+    found, waiting = [], []
 
     def after_block(x0):
         cells = slice(x0 * ny, (x0 + BLOCK) * ny)
         zkin[cells, :] = dot(parts[cells, :], depth_matrix())
-        term = plane_sums(sz, w_ref, parts, x0)
-        found.append(term if not found else found[-1] + term)
+        waiting.append(x0)
+        if len(waiting) == LUMP or x0 + BLOCK == nx:
+            term = plane_sums(sz, w_ref, parts, waiting[0], x0 + BLOCK)
+            found.append(term if not found else found[-1] + term)
+            waiting.clear()
 
     relax_rows(nx, ny, 0, zfield, res, emit_zero, after_block)
     fill_rims(direct, 3, nx, ny)

time: 32.4 us -> 32.4 us (level)
  no operation moved by 1% of the time
where the time goes in v3:
time: 32.4 us; the launch traced here: 32.2 us
  starting transfers between devices  15.3 us (47%)
  Pallas kernels  9.07 us (28%)
  waiting for transfers between devices  7.01 us (22%)
  between operations  0.8 us (2%)
    ppermute x15, starting transfers between devices, gathered(): found.append(lax.ppermute(value, axis, pairs(turn)))  15.3 us
    ppermute x15, waiting for transfers between devices, gathered(): found.append(lax.ppermute(value, axis, pairs(turn)))  7.01 us
    pallas_call x1, Pallas kernels, replicated(): pl.pallas_call(functools.partial(step_kernel, sz), out_shape=(jax.ShapeDt...  4.3 us
    pallas_call x1, Pallas kernels, replicated(): pl.pallas_call(functools.partial(second_kernel, sz), out_shape=(shape(nx,...  1.53 us
    pallas_call x1, Pallas kernels, replicated(): pl.pallas_call(functools.partial(weights_kernel, sz), out_shape=(half(2 *...  1.13 us
    pallas_call x1, Pallas kernels, replicated(): pl.pallas_call(functools.partial(pack_kernel, sz), out_shape=(shape(sz.ro...  1.11 us
    pallas_call x1, Pallas kernels, replicated(): pl.pallas_call(functools.partial(first_kernel, sz), out_shape=(shape(*pad...  1.01 us
  transfers between devices with their start and end apart: 15, of which 5 were waited for; matrix products, arithmetic and copies ran while one was open for 0% of the time, Pallas kernels for 11%

profile of v3, /device:TPU:0, one launch (start us, length us, event | category | flops | bytes accessed | tf_op | source)
XLA Modules:
  0.0 32.2 jit_solution(5608198092079351163)
XLA Ops:
  0.6 1.1 %pack.1 = (f32[40,128]{1,0:T(8,128)S(1)}, f32[1,8,16,128]{3,2,1,0:T(8,128)S(1)}) custom-call(f32[8,16,32]{2,1,0:T(8,128)} %pot_ref.1, s32[1,3,1,4]{3,2,1,0:T(1,128)} %bitcast.5, s32[1,1,4]{2,1,0:T(1,128)} %counts_ref.1, f32[1,1,9,4,9]{4,3,2,1,0:T(4,128)} %bitcast.3, f32[1,1,9,4,9]{4,3,2,1,0:T(4,128)} %bitcast.4, f32[1,8,16,128]{3,2,1,0:T(8,128)} %wave_ref.1), custom_call_target="tpu_custom_call" | custom-call | tf_op jit(solution)/shard_map/pack/pallas_call | solution.py:897
  1.7 3.1 %collective-permute-start = (f32[40,128]{1,0:T(8,128)S(1)}, f32[40,128]{1,0:T(8,128)S(1)}, u32[]{:S(2)}, u32[]{:S(2)}) collective-permute-start(f32[40,128]{1,0:T(8,128)S(1)} %get-tuple-element.15), channel_id=1, source_target_pairs={{2,0},{0,2},{6,4},{4,6},{3,1},{1,3},{7,5},{5,7},{10,8},{8,10},{14,... | collective-permute-start | bytes 61448 | tf_op jit(solution)/shard_map/ppermute | solution.py:876
  4.9 2.6 %collective-permute-start.1 = (f32[40,128]{1,0:T(8,128)S(1)}, f32[40,128]{1,0:T(8,128)S(1)}, u32[]{:S(2)}, u32[]{:S(2)}) collective-permute-start(f32[40,128]{1,0:T(8,128)S(1)} %get-tuple-element.15), channel_id=1, source_target_pairs={{4,0},{6,2},{0,4},{2,6},{5,1},{7,3},{1,5},{3,7},{12,8},{14,10},{8,... | collective-permute-start | bytes 61448 | tf_op jit(solution)/shard_map/ppermute | solution.py:876
  7.5 0.0 collective-permute-start.2
  7.5 0.9 %collective-permute-start.7 = (f32[1,8,16,128]{3,2,1,0:T(8,128)S(1)}, f32[1,8,16,128]{3,2,1,0:T(8,128)S(1)}, u32[]{:S(2)}, u32[]{:S(2)}) collective-permute-start(f32[1,8,16,128]{3,2,1,0:T(8,128)S(1)} %get-tuple-element.16.refs_0_), channel_id=1, source_target_pairs={{2,0},{0,2},{6,4},{4,6},{3,1},{1,3},{7,5},{5,7},{10,8},{8,10},{14,... | collective-permute-start | bytes 196616 | tf_op jit(solution)/shard_map/ppermute | solution.py:876
  8.4 3.5 %collective-permute-start.8 = (f32[1,8,16,128]{3,2,1,0:T(8,128)S(1)}, f32[1,8,16,128]{3,2,1,0:T(8,128)S(1)}, u32[]{:S(2)}, u32[]{:S(2)}) collective-permute-start(f32[1,8,16,128]{3,2,1,0:T(8,128)S(1)} %get-tuple-element.16.refs_0_), channel_id=1, source_target_pairs={{4,0},{6,2},{0,4},{2,6},{5,1},{7,3},{1,5},{3,7},{12,8},{14,10},{8,... | collective-permute-start | bytes 196616 | tf_op jit(solution)/shard_map/ppermute | solution.py:876
  11.8 0.0 collective-permute-done
  11.9 0.1 collective-permute-start.9
  11.9 0.0 collective-permute-done.1
  12.0 0.1 collective-permute-start.10
  12.0 1.0 %collective-permute-done.2 = f32[40,128]{1,0:T(8,128)S(1)} collective-permute-done((f32[40,128]{1,0:T(8,128)S(1)}, f32[40,128]{1,0:T(8,128)S(1)}, u32[]{:S(2)}, u32[]{:S(2)}) %collective-permute-start.2) | collective-permute-done | bytes 20512 | tf_op jit(solution)/shard_map/ppermute | solution.py:876
  13.1 0.0 collective-permute-start.14
  13.1 1.1 %collective-permute-done.14.refs_1_ = f32[32,128]{1,0:T(8,128)S(1)} collective-permute-done((f32[32,128]{1,0:T(8,128)S(1)}, f32[32,128]{1,0:T(8,128)S(1)}, u32[]{:S(2)}, u32[]{:S(2)}) %collective-permute-start.14) | collective-permute-done | bytes 16416 | tf_op jit(solution)/shard_map/ppermute | solution.py:876
  14.3 1.5 %collective-permute-start.3 = (f32[128,128]{1,0:T(8,128)S(1)}, f32[128,128]{1,0:T(8,128)S(1)}, u32[]{:S(2)}, u32[]{:S(2)}) collective-permute-start(f32[128,128]{1,0:T(8,128)S(1)} %pad_maximum_fusion), channel_id=1, source_target_pairs={{8,0},{0,8},{24,16},{16,24},{9,1},{1,9},{25,17},{17,25},{10,2},{2,... | collective-permute-start | bytes 196616 | tf_op jit(solution)/shard_map/ppermute | solution.py:876
  15.8 1.1 %weights.1 = (bf16[640,1024]{1,0:T(8,128)(2,1)S(1)}, bf16[1024,640]{1,0:T(8,128)(2,1)S(1)}, f32[6,32,128]{2,1,0:T(8,128)S(1)}, f32[3,32,128]{2,1,0:T(8,128)S(1)}) custom-call(f32[32,128]{1,0:T(8,128)S(1)} %pad_maximum_fusion.1.refs_0_, f32[32,128]{1,0:T(8,128)S(1)} %collective-permute-done.14.refs_1_), custom_call_target="tpu_custom_call" | custom-call | flops 1000000000 | tf_op jit(solution)/shard_map/weights/pallas_call | solution.py:924
  16.9 1.6 %collective-permute-done.3 = f32[128,128]{1,0:T(8,128)S(1)} collective-permute-done((f32[128,128]{1,0:T(8,128)S(1)}, f32[128,128]{1,0:T(8,128)S(1)}, u32[]{:S(2)}, u32[]{:S(2)}) %collective-permute-start.3) | collective-permute-done | bytes 65568 | tf_op jit(solution)/shard_map/ppermute | solution.py:876
  18.5 1.5 %collective-permute-start.4 = (f32[128,128]{1,0:T(8,128)S(1)}, f32[128,128]{1,0:T(8,128)S(1)}, u32[]{:S(2)}, u32[]{:S(2)}) collective-permute-start(f32[128,128]{1,0:T(8,128)S(1)} %pad_maximum_fusion), channel_id=1, source_target_pairs={{16,0},{24,8},{0,16},{8,24},{17,1},{25,9},{1,17},{9,25},{18,2},{26... | collective-permute-start | bytes 196616 | tf_op jit(solution)/shard_map/ppermute | solution.py:876
  20.1 0.0 collective-permute-done.7.refs_1_
  20.1 1.5 %collective-permute-start.5 = (f32[128,128]{1,0:T(8,128)S(1)}, f32[128,128]{1,0:T(8,128)S(1)}, u32[]{:S(2)}, u32[]{:S(2)}) collective-permute-start(f32[128,128]{1,0:T(8,128)S(1)} %pad_maximum_fusion), channel_id=1, source_target_pairs={{24,0},{16,8},{8,16},{0,24},{25,1},{17,9},{9,17},{1,25},{26,2},{18... | collective-permute-start | bytes 196616 | tf_op jit(solution)/shard_map/ppermute | solution.py:876
  21.6 0.0 collective-permute-done.8.refs_2_
  21.6 0.0 collective-permute-start.11
  21.6 0.0 collective-permute-done.9.refs_3_
  21.6 0.5 %collective-permute-start.12 = (f32[1,8,16,128]{3,2,1,0:T(8,128)S(1)}, f32[1,8,16,128]{3,2,1,0:T(8,128)S(1)}, u32[]{:S(2)}, u32[]{:S(2)}) collective-permute-start(f32[1,8,16,128]{3,2,1,0:T(8,128)S(1)} %collective-permute-done.8.refs_2_), channel_id=1, source_target_pairs={{1,0},{0,1},{3,2},{2,3},{5,4},{4,5},{7,6},{6,7},{9,8},{8,9},{11,10... | collective-permute-start | bytes 196616 | tf_op jit(solution)/shard_map/ppermute | solution.py:876
  22.1 1.4 %collective-permute-done.4 = f32[128,128]{1,0:T(8,128)S(1)} collective-permute-done((f32[128,128]{1,0:T(8,128)S(1)}, f32[128,128]{1,0:T(8,128)S(1)}, u32[]{:S(2)}, u32[]{:S(2)}) %collective-permute-start.4) | collective-permute-done | bytes 65568 | tf_op jit(solution)/shard_map/ppermute | solution.py:876
  23.5 0.0 collective-permute-start.13
  23.5 1.8 %collective-permute-done.5 = f32[128,128]{1,0:T(8,128)S(1)} collective-permute-done((f32[128,128]{1,0:T(8,128)S(1)}, f32[128,128]{1,0:T(8,128)S(1)}, u32[]{:S(2)}, u32[]{:S(2)}) %collective-permute-start.5) | collective-permute-done | bytes 65568 | tf_op jit(solution)/shard_map/ppermute | solution.py:876
  25.3 0.0 collective-permute-start.6
  25.3 0.0 collective-permute-done.10.refs_4_
  25.3 0.0 collective-permute-done.11.refs_5_
  25.3 0.0 collective-permute-done.12.refs_6_
  25.3 0.0 collective-permute-done.13.refs_7_
  25.3 1.0 %first.1 = (f32[38,48,128]{2,1,0:T(8,128)S(1)}, f32[1024,128]{1,0:T(8,128)S(1)}, f32[32,128]{1,0:T(8,128)S(1)}) custom-call(f32[1,8,16,128]{3,2,1,0:T(8,128)S(1)} %get-tuple-element.16.refs_0_, f32[1,8,16,128]{3,2,1,0:T(8,128)S(1)} %collective-permute-done.7.refs_1_, f32[1,8,16,128]{3,2,1,0:T(8,128)S(1)} %collective-permute-done.8.refs_2_, ...), custom_call_target="tpu_custom_call" | custom-call | flops 2000000000 | tf_op jit(solution)/shard_map/first/pallas_call | solution.py:939
  26.4 1.5 %second.1 = (f32[32,32,128]{2,1,0:T(8,128)S(1)}, f32[32,32,128]{2,1,0:T(8,128)S(1)}, f32[2,128]{1,0:T(2,128)S(1)}) custom-call(f32[38,48,128]{2,1,0:T(8,128)S(1)} %get-tuple-element.20.refs_0_.refs_2_, f32[1024,128]{1,0:T(8,128)S(1)} %get-tuple-element.21.refs_1_, f32[32,128]{1,0:T(8,128)S(1)} %get-tuple-element.22.refs_2_, ...), custom_call_target="tpu_custom_call" | custom-call | flops 2000000000 | tf_op jit(solution)/shard_map/second/pallas_call | solution.py:949
  27.9 0.0 collective-permute-done.6.refs_1_
  27.9 4.3 %step.1 = (f32[1,8,16,128]{3,2,1,0:T(8,128)}, f32[1,8,16,128]{3,2,1,0:T(8,128)}, f32[1]{0:T(128)}) custom-call(f32[512,128]{1,0:T(8,128)S(1)} %constant_dynamic-update-slice_fusion.refs_0_, f32[512,128]{1,0:T(8,128)S(1)} %collective-permute-done.6.refs_1_, f32[38,48,128]{2,1,0:T(8,128)S(1)} %get-tuple-element.20.refs_0_.refs_2_, ...), custom_call_target="tpu_custom_call" | custom-call | flops 6000000000 | tf_op jit(solution)/shard_map/step/pallas_call | solution.py:960
  (13 shorter events, 0.1 us)
Async XLA Ops:
  1.7 10.1 %collective-permute-start = (f32[40,128]{1,0:T(8,128)S(1)}, f32[40,128]{1,0:T(8,128)S(1)}, u32[]{:S(2)}, u32[]{:S(2)}) collective-permute-start(f32[40,128]{1,0:T(8,128)S(1)} %get-tuple-element.15), channel_id=1, source_target_pairs={{2,0},{0,2},{6,4},{4,6},{3,1},{1,3},{7,5},{5,7},{10,8},{8,10},{14,... | collective-permute-start | bytes 61448 | tf_op jit(solution)/shard_map/ppermute | solution.py:876
  4.9 7.1 %collective-permute-start.1 = (f32[40,128]{1,0:T(8,128)S(1)}, f32[40,128]{1,0:T(8,128)S(1)}, u32[]{:S(2)}, u32[]{:S(2)}) collective-permute-start(f32[40,128]{1,0:T(8,128)S(1)} %get-tuple-element.15), channel_id=1, source_target_pairs={{4,0},{6,2},{0,4},{2,6},{5,1},{7,3},{1,5},{3,7},{12,8},{14,10},{8,... | collective-permute-start | bytes 61448 | tf_op jit(solution)/shard_map/ppermute | solution.py:876
  7.5 5.6 %collective-permute-start.2 = (f32[40,128]{1,0:T(8,128)S(1)}, f32[40,128]{1,0:T(8,128)S(1)}, u32[]{:S(2)}, u32[]{:S(2)}) collective-permute-start(f32[40,128]{1,0:T(8,128)S(1)} %get-tuple-element.15), channel_id=1, source_target_pairs={{6,0},{4,2},{2,4},{0,6},{7,1},{5,3},{3,5},{1,7},{14,8},{12,10},{10... | collective-permute-start | bytes 61448 | tf_op jit(solution)/shard_map/ppermute | solution.py:876
  7.5 12.6 %collective-permute-start.7 = (f32[1,8,16,128]{3,2,1,0:T(8,128)S(1)}, f32[1,8,16,128]{3,2,1,0:T(8,128)S(1)}, u32[]{:S(2)}, u32[]{:S(2)}) collective-permute-start(f32[1,8,16,128]{3,2,1,0:T(8,128)S(1)} %get-tuple-element.16.refs_0_), channel_id=1, source_target_pairs={{2,0},{0,2},{6,4},{4,6},{3,1},{1,3},{7,5},{5,7},{10,8},{8,10},{14,... | collective-permute-start | bytes 196616 | tf_op jit(solution)/shard_map/ppermute | solution.py:876
  8.4 13.2 %collective-permute-start.8 = (f32[1,8,16,128]{3,2,1,0:T(8,128)S(1)}, f32[1,8,16,128]{3,2,1,0:T(8,128)S(1)}, u32[]{:S(2)}, u32[]{:S(2)}) collective-permute-start(f32[1,8,16,128]{3,2,1,0:T(8,128)S(1)} %get-tuple-element.16.refs_0_), channel_id=1, source_target_pairs={{4,0},{6,2},{0,4},{2,6},{5,1},{7,3},{1,5},{3,7},{12,8},{14,10},{8,... | collective-permute-start | bytes 196616 | tf_op jit(solution)/shard_map/ppermute | solution.py:876
  11.9 9.7 %collective-permute-start.9 = (f32[1,8,16,128]{3,2,1,0:T(8,128)S(1)}, f32[1,8,16,128]{3,2,1,0:T(8,128)S(1)}, u32[]{:S(2)}, u32[]{:S(2)}) collective-permute-start(f32[1,8,16,128]{3,2,1,0:T(8,128)S(1)} %get-tuple-element.16.refs_0_), channel_id=1, source_target_pairs={{6,0},{4,2},{2,4},{0,6},{7,1},{5,3},{3,5},{1,7},{14,8},{12,10},{10... | collective-permute-start | bytes 196616 | tf_op jit(solution)/shard_map/ppermute | solution.py:876
  12.0 13.3 %collective-permute-start.10 = (f32[1,8,16,128]{3,2,1,0:T(8,128)S(1)}, f32[1,8,16,128]{3,2,1,0:T(8,128)S(1)}, u32[]{:S(2)}, u32[]{:S(2)}) collective-permute-start(f32[1,8,16,128]{3,2,1,0:T(8,128)S(1)} %get-tuple-element.16.refs_0_), channel_id=1, source_target_pairs={{1,0},{0,1},{3,2},{2,3},{5,4},{4,5},{7,6},{6,7},{9,8},{8,9},{11,10... | collective-permute-start | bytes 196616 | tf_op jit(solution)/shard_map/ppermute | solution.py:876
  13.1 1.2 %collective-permute-start.14 = (f32[32,128]{1,0:T(8,128)S(1)}, f32[32,128]{1,0:T(8,128)S(1)}, u32[]{:S(2)}, u32[]{:S(2)}) collective-permute-start(f32[32,128]{1,0:T(8,128)S(1)} %pad_maximum_fusion.1.refs_0_), channel_id=1, source_target_pairs={{1,0},{0,1},{3,2},{2,3},{5,4},{4,5},{7,6},{6,7},{9,8},{8,9},{11,10... | collective-permute-start | bytes 49160 | tf_op jit(solution)/shard_map/ppermute | solution.py:876
  14.3 4.3 %collective-permute-start.3 = (f32[128,128]{1,0:T(8,128)S(1)}, f32[128,128]{1,0:T(8,128)S(1)}, u32[]{:S(2)}, u32[]{:S(2)}) collective-permute-start(f32[128,128]{1,0:T(8,128)S(1)} %pad_maximum_fusion), channel_id=1, source_target_pairs={{8,0},{0,8},{24,16},{16,24},{9,1},{1,9},{25,17},{17,25},{10,2},{2,... | collective-permute-start | bytes 196616 | tf_op jit(solution)/shard_map/ppermute | solution.py:876
  18.5 5.0 %collective-permute-start.4 = (f32[128,128]{1,0:T(8,128)S(1)}, f32[128,128]{1,0:T(8,128)S(1)}, u32[]{:S(2)}, u32[]{:S(2)}) collective-permute-start(f32[128,128]{1,0:T(8,128)S(1)} %pad_maximum_fusion), channel_id=1, source_target_pairs={{16,0},{24,8},{0,16},{8,24},{17,1},{25,9},{1,17},{9,25},{18,2},{26... | collective-permute-start | bytes 196616 | tf_op jit(solution)/shard_map/ppermute | solution.py:876
  20.1 5.2 %collective-permute-start.5 = (f32[128,128]{1,0:T(8,128)S(1)}, f32[128,128]{1,0:T(8,128)S(1)}, u32[]{:S(2)}, u32[]{:S(2)}) collective-permute-start(f32[128,128]{1,0:T(8,128)S(1)} %pad_maximum_fusion), channel_id=1, source_target_pairs={{24,0},{16,8},{8,16},{0,24},{25,1},{17,9},{9,17},{1,25},{26,2},{18... | collective-permute-start | bytes 196616 | tf_op jit(solution)/shard_map/ppermute | solution.py:876
  21.6 3.8 %collective-permute-start.11 = (f32[1,8,16,128]{3,2,1,0:T(8,128)S(1)}, f32[1,8,16,128]{3,2,1,0:T(8,128)S(1)}, u32[]{:S(2)}, u32[]{:S(2)}) collective-permute-start(f32[1,8,16,128]{3,2,1,0:T(8,128)S(1)} %collective-permute-done.7.refs_1_), channel_id=1, source_target_pairs={{1,0},{0,1},{3,2},{2,3},{5,4},{4,5},{7,6},{6,7},{9,8},{8,9},{11,10... | collective-permute-start | bytes 196616 | tf_op jit(solution)/shard_map/ppermute | solution.py:876
  21.6 3.8 %collective-permute-start.12 = (f32[1,8,16,128]{3,2,1,0:T(8,128)S(1)}, f32[1,8,16,128]{3,2,1,0:T(8,128)S(1)}, u32[]{:S(2)}, u32[]{:S(2)}) collective-permute-start(f32[1,8,16,128]{3,2,1,0:T(8,128)S(1)} %collective-permute-done.8.refs_2_), channel_id=1, source_target_pairs={{1,0},{0,1},{3,2},{2,3},{5,4},{4,5},{7,6},{6,7},{9,8},{8,9},{11,10... | collective-permute-start | bytes 196616 | tf_op jit(solution)/shard_map/ppermute | solution.py:876
  23.5 1.8 %collective-permute-start.13 = (f32[1,8,16,128]{3,2,1,0:T(8,128)S(1)}, f32[1,8,16,128]{3,2,1,0:T(8,128)S(1)}, u32[]{:S(2)}, u32[]{:S(2)}) collective-permute-start(f32[1,8,16,128]{3,2,1,0:T(8,128)S(1)} %collective-permute-done.9.refs_3_), channel_id=1, source_target_pairs={{1,0},{0,1},{3,2},{2,3},{5,4},{4,5},{7,6},{6,7},{9,8},{8,9},{11,10... | collective-permute-start | bytes 196616 | tf_op jit(solution)/shard_map/ppermute | solution.py:876
  25.3 2.6 %collective-permute-start.6 = (f32[512,128]{1,0:T(8,128)S(1)}, f32[512,128]{1,0:T(8,128)S(1)}, u32[]{:S(2)}, u32[]{:S(2)}) collective-permute-start(f32[512,128]{1,0:T(8,128)S(1)} %constant_dynamic-update-slice_fusion.refs_0_), channel_id=1, source_target_pairs={{1,0},{0,1},{3,2},{2,3},{5,4},{4,5},{7,6},{6,7},{9,8},{8,9},{11,10... | collective-permute-start | bytes 786440 | tf_op jit(solution)/shard_map/ppermute | solution.py:876
